TPU v7x, 32 devices: a whole 2x2x4 slice. The times are simulated.
32 devices in a mesh: dp: 8 (over y, x, core), tensor: 4 (over z).
Axes of the slice: x: 2, y: 2, z: 4, core: 2. Of those that a mesh axis runs over, the one named last changes fastest.
Arguments:
- activations: bfloat16 [16, 1024, 1024], P('dp', 'tensor'), may hold values from -6 to 6
- cotangent: bfloat16 [16, 1024, 1024], P('dp', 'tensor'), may hold values from -6 to 6
- attn_gain: float32 [1024], replicated, may hold values from 0.5 to 1.5
- attn_shift: float32 [1024], replicated, may hold values from -2 to 2
- qkv_weight: bfloat16 [1024, 3072], P('dp', 'tensor'), may hold values from -0.1875 to 0.1875
- qkv_bias: float32 [3072], P('tensor'), may hold values from -3 to 3
- out_weight: bfloat16 [1024, 1024], P('dp', 'tensor'), may hold values from -3.5 to 3.5
- out_bias: float32 [1024], replicated, may hold values from -2 to 2
- mlp_gain: float32 [1024], replicated, may hold values from 0.5 to 1.5
- mlp_shift: float32 [1024], replicated, may hold values from -2 to 2
- fc1_weight: bfloat16 [1024, 4096], P('dp', 'tensor'), may hold values from -0.1875 to 0.1875
- fc1_bias: float32 [4096], P('tensor'), may hold values from -3 to 3
- fc2_weight: bfloat16 [1024, 4096], P('dp', 'tensor'), may hold values from -0.09375 to 0.09375
- fc2_bias: float32 [1024], replicated, may hold values from -2 to 2
Outputs:
- output: bfloat16 [16, 1024, 1024], P('dp', 'tensor')
- input_grad: float32 [16, 1024, 1024], P('dp', 'tensor')
- grad_attn_gain: float32 [1024], replicated
- grad_attn_shift: float32 [1024], replicated
- grad_qkv_weight: float32 [1024, 3072], P('dp', 'tensor')
- grad_qkv_bias: float32 [3072], P('tensor')
- grad_out_weight: float32 [1024, 1024], P('dp', 'tensor')
- grad_out_bias: float32 [1024], replicated
- grad_mlp_gain: float32 [1024], replicated
- grad_mlp_shift: float32 [1024], replicated
- grad_fc1_weight: float32 [1024, 4096], P('dp', 'tensor')
- grad_fc1_bias: float32 [4096], P('tensor')
- grad_fc2_weight: float32 [1024, 4096], P('dp', 'tensor')
- grad_fc2_bias: float32 [1024], replicated
All inputs are finite; a program needn't handle non-finite values.
Results may differ from a plain program's by a relative error of at most 0.02.
Values may be sent and summed in bfloat16 or wider, within the bound.
No kernel may reach another device: no remote copies, remote signals or barrier semaphores. Data moves between devices by JAX's collectives and lax.ppermute only.
A program may use at most 192 MiB of HBM per device.

v0:
```python
import math

import jax
import jax.numpy as jnp
from jax import lax
from jax.sharding import PartitionSpec as P

HD = 64
GRID = 16


def norm_rows(values, gain_vec, shift_vec):
    row_mean = jnp.mean(values, axis=-1, keepdims=True)
    centred = values - row_mean
    variance = jnp.mean(centred * centred, axis=-1, keepdims=True)
    return centred * lax.rsqrt(variance + 1e-06) * gain_vec + shift_vec


def rotary_tables(length):
    section = 2 * (HD // 3 // 2)
    half = section // 2
    position = jnp.arange(length)
    frame = (position // (GRID * GRID)).astype(jnp.float32)
    row_pos = (position // GRID % GRID).astype(jnp.float32)
    col_pos = (position % GRID).astype(jnp.float32)
    omega = 1.0 / 10000.0 ** (jnp.arange(half).astype(jnp.float32) / half)
    pieces = [
        jnp.repeat(coordinate[:, None] * omega[None, :], 2, axis=1)
        for coordinate in (frame, row_pos, col_pos)
    ]
    pieces.append(jnp.zeros((length, HD - 3 * section), jnp.float32))
    angles = jnp.concatenate(pieces, axis=1)
    parity = jnp.where(jnp.arange(HD) % 2 == 0, -1.0, 1.0).astype(jnp.float32)
    return (jnp.cos(angles), jnp.sin(angles) * parity)


def pair_swap(values):
    shape = values.shape
    paired = values.reshape(shape[:-1] + (shape[-1] // 2, 2))
    return paired[..., ::-1].reshape(shape)


def contract(left, right, left_dim, right_dim):
    return lax.dot_general(
        left, right, (((left_dim,), (right_dim,)), ((), ())), preferred_element_type=jnp.float32
    )


def exact_gelu(values):
    return jax.nn.gelu(values, approximate=False)


def body(
    activations,
    cotangent,
    attn_gain,
    attn_shift,
    qkv_weight,
    qkv_bias,
    out_weight,
    out_bias,
    mlp_gain,
    mlp_shift,
    fc1_weight,
    fc1_bias,
    fc2_weight,
    fc2_bias,
):
    tensor_size = lax.axis_size("tensor")
    tensor_rank = lax.axis_index("tensor")
    row_count = activations.shape[1]
    width = activations.shape[2]
    length = row_count * tensor_size
    block_rows = min(512, length)
    block_count = length // block_rows
    local_heads = qkv_weight.shape[1] // (3 * HD)
    packed_cols = qkv_weight.shape[1]
    unit_cols = fc1_weight.shape[1]
    factor = 1.0 / math.sqrt(HD)
    cosine, sine = rotary_tables(length)
    cosine = cosine[:, None, :]
    sine = sine[:, None, :]

    def rotate(values):
        return values * cosine + pair_swap(values) * sine

    def rotate_back(values):
        return values * cosine + pair_swap(values * sine)

    def fetch():
        gathered = (
            lax.all_gather(qkv_weight, "dp", axis=0, tiled=True),
            lax.all_gather(out_weight, "dp", axis=0, tiled=True),
            lax.all_gather(fc1_weight, "dp", axis=0, tiled=True),
            lax.all_gather(fc2_weight, "dp", axis=0, tiled=True),
        )
        return (gathered, gathered)

    def seq_gather(values):
        return lax.all_gather(values, "tensor", axis=0, tiled=True)

    def part_sum(values):
        return lax.psum_scatter(
            values.astype(jnp.bfloat16), "tensor", scatter_dimension=0, tiled=True
        ).astype(jnp.float32)

    def grad_gather(values):
        return lax.all_gather(values, "tensor", axis=0, tiled=True)

    def grad_sum(values):
        return lax.psum_scatter(
            values.astype(jnp.bfloat16), "tensor", scatter_dimension=0, tiled=True
        ).astype(jnp.float32)

    def forward(inputs, weights):
        (weight_qkv, weight_out, weight_up, weight_down), (
            whole_qkv,
            whole_out,
            whole_up,
            whole_down,
        ) = weights
        first_all = seq_gather(norm_rows(inputs, attn_gain, attn_shift).astype(jnp.bfloat16))
        packed = (
            jnp.dot(first_all, weight_qkv, preferred_element_type=jnp.float32) + qkv_bias
        ).reshape(length, local_heads, 3, HD)
        query = rotate(packed[:, :, 0]).astype(jnp.bfloat16)
        key_all = rotate(packed[:, :, 1]).astype(jnp.bfloat16)
        value_all = packed[:, :, 2].astype(jnp.bfloat16)
        outputs = []
        log_sums = []
        for block in range(block_count):
            query_block = query[block * block_rows : (block + 1) * block_rows]
            scores = (
                jnp.einsum("qhd,khd->hqk", query_block, key_all, preferred_element_type=jnp.float32)
                * factor
            )
            row_max = jnp.max(scores, axis=-1, keepdims=True)
            expo = jnp.exp(scores - row_max)
            row_total = jnp.sum(expo, axis=-1, keepdims=True)
            weights_low = (expo / row_total).astype(jnp.bfloat16)
            outputs.append(
                jnp.einsum(
                    "hqk,khd->qhd", weights_low, value_all, preferred_element_type=jnp.float32
                )
            )
            log_sums.append(row_max + jnp.log(row_total))
        heads_out = (
            jnp.concatenate(outputs, axis=0).reshape(length, local_heads * HD).astype(jnp.bfloat16)
        )
        log_total = jnp.concatenate(log_sums, axis=1)
        attended = part_sum(contract(heads_out, weight_out, 1, 1))
        resid = inputs + attended + out_bias
        second_all = seq_gather(norm_rows(resid, mlp_gain, mlp_shift).astype(jnp.bfloat16))
        hidden = jnp.dot(second_all, weight_up, preferred_element_type=jnp.float32) + fc1_bias
        act = exact_gelu(hidden).astype(jnp.bfloat16)
        branch = part_sum(contract(act, weight_down, 1, 1))
        result = resid + branch + fc2_bias
        kept = (
            first_all,
            query,
            key_all,
            value_all,
            log_total,
            heads_out,
            heads_out,
            resid,
            second_all,
            hidden,
            act,
        )
        return (result, kept)

    def backward(inputs, grad_low, kept, weights):
        (weight_qkv, weight_out, weight_up, weight_down), (
            whole_qkv,
            whole_out,
            whole_up,
            whole_down,
        ) = weights
        (
            first_all,
            query,
            key_all,
            value_all,
            log_total,
            heads_out,
            heads_rows,
            resid,
            second_all,
            hidden,
            act,
        ) = kept
        grad_top = grad_low.astype(jnp.float32)
        grad_fc2_bias = jnp.sum(grad_top, axis=0)
        grad_all = grad_gather(grad_low)
        grad_fc2_weight = contract(grad_all, act, 0, 0)
        grad_act = jnp.dot(grad_all, weight_down, preferred_element_type=jnp.float32)
        gelu_pull = jax.vjp(exact_gelu, hidden)[1]
        grad_hidden = gelu_pull(grad_act)[0].astype(jnp.bfloat16)
        grad_fc1_bias = jnp.sum(grad_hidden, axis=0, dtype=jnp.float32)
        grad_fc1_weight = contract(second_all, grad_hidden, 0, 0)
        grad_second = grad_sum(contract(grad_hidden, weight_up, 1, 1))
        second_pull = jax.vjp(norm_rows, resid, mlp_gain, mlp_shift)[1]
        grad_resid_norm, grad_mlp_gain, grad_mlp_shift = second_pull(grad_second)
        grad_resid = grad_top + grad_resid_norm
        grad_out_bias = jnp.sum(grad_resid, axis=0)
        resid_low = grad_resid.astype(jnp.bfloat16)
        resid_all = grad_gather(resid_low)
        grad_out_weight = contract(resid_all, heads_out, 0, 0)
        grad_heads = jnp.dot(resid_all, weight_out, preferred_element_type=jnp.float32).astype(
            jnp.bfloat16
        )
        grad_heads = grad_heads.reshape(length, local_heads, HD)
        grad_key = jnp.zeros((length, local_heads, HD), jnp.float32)
        grad_value = jnp.zeros((length, local_heads, HD), jnp.float32)
        query_grads = []
        for block in range(block_count):
            lower = block * block_rows
            upper = lower + block_rows
            query_block = query[lower:upper]
            grad_block = grad_heads[lower:upper]
            scores = (
                jnp.einsum("qhd,khd->hqk", query_block, key_all, preferred_element_type=jnp.float32)
                * factor
            )
            probs = jnp.exp(scores - log_total[:, lower:upper])
            grad_value = grad_value + jnp.einsum(
                "hqk,qhd->khd",
                probs.astype(jnp.bfloat16),
                grad_block,
                preferred_element_type=jnp.float32,
            )
            grad_probs = jnp.einsum(
                "qhd,khd->hqk", grad_block, value_all, preferred_element_type=jnp.float32
            )
            grad_scores = (
                probs * (grad_probs - jnp.sum(probs * grad_probs, axis=-1, keepdims=True))
            ).astype(jnp.bfloat16)
            query_grads.append(
                jnp.einsum("hqk,khd->qhd", grad_scores, key_all, preferred_element_type=jnp.float32)
                * factor
            )
            grad_key = (
                grad_key
                + jnp.einsum(
                    "hqk,qhd->khd", grad_scores, query_block, preferred_element_type=jnp.float32
                )
                * factor
            )
        grad_query = jnp.concatenate(query_grads, axis=0)
        grad_packed = jnp.stack(
            [rotate_back(grad_query), rotate_back(grad_key), grad_value], axis=2
        )
        grad_packed = grad_packed.reshape(length, packed_cols).astype(jnp.bfloat16)
        grad_qkv_bias = jnp.sum(grad_packed, axis=0, dtype=jnp.float32)
        grad_qkv_weight = contract(first_all, grad_packed, 0, 0)
        grad_first = grad_sum(contract(grad_packed, weight_qkv, 1, 1))
        first_pull = jax.vjp(norm_rows, inputs, attn_gain, attn_shift)[1]
        grad_input_norm, grad_attn_gain, grad_attn_shift = first_pull(grad_first)
        input_grad = grad_resid + grad_input_norm
        grads = (
            grad_attn_gain,
            grad_attn_shift,
            grad_qkv_weight,
            grad_qkv_bias,
            grad_out_weight,
            grad_out_bias,
            grad_mlp_gain,
            grad_mlp_shift,
            grad_fc1_weight,
            grad_fc1_bias,
            grad_fc2_weight,
            grad_fc2_bias,
        )
        return (input_grad, grads)

    def per_clip(totals, inputs_pair):
        clip_in, clip_grad = inputs_pair
        forward_weights = fetch()
        result, kept = forward(clip_in.astype(jnp.float32), forward_weights)
        backward_weights = fetch()
        input_grad, grads = backward(clip_in.astype(jnp.float32), clip_grad, kept, backward_weights)
        totals = tuple((left + right for left, right in zip(totals, grads)))
        return (totals, (result.astype(jnp.bfloat16), input_grad))

    out_cols = local_heads * HD
    start_totals = (
        jnp.zeros((width,), jnp.float32),
        jnp.zeros((width,), jnp.float32),
        jnp.zeros((width, packed_cols), jnp.float32),
        jnp.zeros((packed_cols,), jnp.float32),
        jnp.zeros((width, out_cols), jnp.float32),
        jnp.zeros((width,), jnp.float32),
        jnp.zeros((width,), jnp.float32),
        jnp.zeros((width,), jnp.float32),
        jnp.zeros((width, unit_cols), jnp.float32),
        jnp.zeros((unit_cols,), jnp.float32),
        jnp.zeros((width, unit_cols), jnp.float32),
        jnp.zeros((width,), jnp.float32),
    )
    totals, (output, input_grad) = lax.scan(per_clip, start_totals, (activations, cotangent))
    out_grad = totals[4]
    weight_sums = (
        lax.psum_scatter(
            totals[2].astype(jnp.bfloat16), "dp", scatter_dimension=0, tiled=True
        ).astype(jnp.float32),
        lax.psum_scatter(
            out_grad.astype(jnp.bfloat16), "dp", scatter_dimension=0, tiled=True
        ).astype(jnp.float32),
        lax.psum_scatter(
            totals[8].astype(jnp.bfloat16), "dp", scatter_dimension=0, tiled=True
        ).astype(jnp.float32),
        lax.psum_scatter(
            totals[10].astype(jnp.bfloat16), "dp", scatter_dimension=0, tiled=True
        ).astype(jnp.float32),
    )
    qkv_place = lax.dynamic_update_slice_in_dim(
        jnp.zeros((packed_cols * tensor_size,), jnp.float32),
        totals[3],
        tensor_rank * packed_cols,
        0,
    )
    unit_place = lax.dynamic_update_slice_in_dim(
        jnp.zeros((unit_cols * tensor_size,), jnp.float32), totals[9], tensor_rank * unit_cols, 0
    )
    summed = lax.psum(
        (totals[0], totals[1], qkv_place, totals[5], totals[6], totals[7], unit_place, totals[11]),
        ("dp", "tensor"),
    )
    grad_qkv_bias = lax.dynamic_slice_in_dim(summed[2], tensor_rank * packed_cols, packed_cols, 0)
    grad_fc1_bias = lax.dynamic_slice_in_dim(summed[6], tensor_rank * unit_cols, unit_cols, 0)
    return (
        output,
        input_grad,
        summed[0],
        summed[1],
        weight_sums[0],
        grad_qkv_bias,
        weight_sums[1],
        summed[3],
        summed[4],
        summed[5],
        weight_sums[2],
        grad_fc1_bias,
        weight_sums[3],
        summed[7],
    )


def solution(mesh):
    in_specs = (
        P("dp", "tensor", None),
        P("dp", "tensor", None),
        P(),
        P(),
        P("dp", "tensor"),
        P("tensor"),
        P("dp", "tensor"),
        P(),
        P(),
        P(),
        P("dp", "tensor"),
        P("tensor"),
        P("dp", "tensor"),
        P(),
    )
    out_specs = (
        P("dp", "tensor", None),
        P("dp", "tensor", None),
        P(),
        P(),
        P("dp", "tensor"),
        P("tensor"),
        P("dp", "tensor"),
        P(),
        P(),
        P(),
        P("dp", "tensor"),
        P("tensor"),
        P("dp", "tensor"),
        P(),
    )
    return jax.shard_map(body, mesh=mesh, in_specs=in_specs, out_specs=out_specs, check_vma=False)
```

profile of v0, /device:TPU:1, one launch (start us, length us, event | category | flops | bytes accessed | tf_op | source)
XLA Modules:
  0.0 1280.8 jit_solution(289971395987647129)
XLA Ops:
  12.3 1091.1 %while.38 = (s32[]{:T(128)}, f32[1024]{0:T(1024)}, f32[1024]{0:T(1024)}, f32[1024,768]{1,0:T(8,128)}, f32[768]{0:T(1024)}, /*index=5*/f32[1024,256]{1,0:T(8,128)...) while((s32[]{:T(128)}, f32[1024]{0:T(1024)}, ...), condition=%wide.wide.region_27.28_spmd.clone, body=%wide.wide.region_0.27_spmd.clone.sunk | while | flops 22775205888 | bytes 743322112 | solution.py:301
  44.4 47.3 %all-gather.13.cloned.1.call-done = bf16[1024,1024]{1,0:T(8,128)(2,1)} async-done(((bf16[256,1024]{1,0:T(8,128)(2,1)}), bf16[1024,1024]{1,0:T(8,128)(2,1)}) %all-gather.13.cloned.1.call-update) | async-done | bytes 2097168 | tf_op jit(solution)/shard_map/while/body/eval_jaxpr/all_gather | solution.py:100
  134.0 41.7 %reduce-scatter.17.cloned.1.call-done = bf16[256,1024]{1,0:T(8,128)(2,1)} async-done(((bf16[1024,1024]{1,0:T(8,128)(2,1)}), bf16[256,1024]{1,0:T(8,128)(2,1)}) %reduce-scatter.17.cloned.1.call-update) | async-done | bytes 524304 | tf_op jit(solution)/shard_map/while/body/eval_jaxpr/reduce_scatter | solution.py:103
  182.4 22.9 %all-gather.19.cloned.1.call-done = bf16[1024,1024]{1,0:T(8,128)(2,1)} async-done(((bf16[128,1024]{1,0:T(8,128)(2,1)}), bf16[1024,1024]{1,0:T(8,128)(2,1)}) %all-gather.19.cloned.1.call-update) | async-done | bytes 2097168 | tf_op jit(solution)/shard_map/while/body/eval_jaxpr/all_gather | solution.py:94
  205.3 47.1 %all-gather.17.cloned.1.call-done = bf16[1024,1024]{1,0:T(8,128)(2,1)} async-done(((bf16[256,1024]{1,0:T(8,128)(2,1)}), bf16[1024,1024]{1,0:T(8,128)(2,1)}) %all-gather.17.cloned.1.call-update) | async-done | bytes 2097168 | tf_op jit(solution)/shard_map/while/body/eval_jaxpr/all_gather | solution.py:100
  252.4 15.4 %multiply_convert_fusion.9 = (bf16[1024,1024]{1,0:T(8,128)(2,1)}, f32[1024,1024]{1,0:T(8,128)}, f32[1024,1024]{1,0:T(8,128)}) fusion(f32[1024]{0:T(1024)S(1)} %copy-done.66, bf16[1024,1024]{1,0:T(8,128)(2,1)} %all-gather.17.cloned.1.call-done, bf16[1024,1024]{1,0:T(8,128)(2,1)} %all-gather.19.cloned.1.call-done), kind=kOutput, calls=%fused_computation.22.clone.clone.1 | convolution fusion | flops 2216689664 | bytes 14684160 | tf_op jit(solution)/shard_map/while/body/eval_jaxpr/dot_general | solution.py:154
  267.8 31.1 %all-gather.23.cloned.1.call-done = bf16[1,1024,1024]{2,1,0:T(8,128)(2,1)} async-done(((bf16[1,256,1024]{2,1,0:T(8,128)(2,1)}), bf16[1,1024,1024]{2,1,0:T(8,128)(2,1)}) %all-gather.23.cloned.1.call-update) | async-done | bytes 2097168 | tf_op jit(solution)/shard_map/while/body/eval_jaxpr/all_gather | solution.py:108
  298.9 29.1 %all-gather.21.cloned.1.call-done = bf16[1024,1024]{1,0:T(8,128)(2,1)} async-done(((bf16[128,1024]{1,0:T(8,128)(2,1)}), bf16[1024,1024]{1,0:T(8,128)(2,1)}) %all-gather.21.cloned.1.call-update) | async-done | bytes 2097168 | tf_op jit(solution)/shard_map/while/body/eval_jaxpr/all_gather | solution.py:95
  341.5 42.9 %reduce-scatter.19.cloned.1.call-done = bf16[256,1024]{1,0:T(8,128)(2,1)} async-done(((bf16[1024,1024]{1,0:T(8,128)(2,1)}), bf16[256,1024]{1,0:T(8,128)(2,1)}) %reduce-scatter.19.cloned.1.call-update) | async-done | bytes 524304 | tf_op jit(solution)/shard_map/while/body/eval_jaxpr/reduce_scatter | solution.py:111
  399.3 37.1 %all-gather.25.cloned.1.call-done = bf16[1024,1024]{1,0:T(8,128)(2,1)} async-done(((bf16[256,1024]{1,0:T(8,128)(2,1)}), bf16[1024,1024]{1,0:T(8,128)(2,1)}) %all-gather.25.cloned.1.call-update) | async-done | bytes 2097168 | tf_op jit(solution)/shard_map/while/body/eval_jaxpr/all_gather | solution.py:108
  529.4 22.6 %reduce-scatter.21.cloned.1.call-done = bf16[256,1024]{1,0:T(8,128)(2,1)} async-done(((bf16[1024,1024]{1,0:T(8,128)(2,1)}), bf16[256,1024]{1,0:T(8,128)(2,1)}) %reduce-scatter.21.cloned.1.call-update) | async-done | bytes 524304 | tf_op jit(solution)/shard_map/while/body/eval_jaxpr/reduce_scatter | solution.py:111
  587.3 47.3 %all-gather.13.cloned.1.call-done = bf16[1024,1024]{1,0:T(8,128)(2,1)} async-done(((bf16[256,1024]{1,0:T(8,128)(2,1)}), bf16[1024,1024]{1,0:T(8,128)(2,1)}) %all-gather.13.cloned.1.call-update) | async-done | bytes 2097168 | tf_op jit(solution)/shard_map/while/body/eval_jaxpr/all_gather | solution.py:100
  677.0 41.7 %reduce-scatter.17.cloned.1.call-done = bf16[256,1024]{1,0:T(8,128)(2,1)} async-done(((bf16[1024,1024]{1,0:T(8,128)(2,1)}), bf16[256,1024]{1,0:T(8,128)(2,1)}) %reduce-scatter.17.cloned.1.call-update) | async-done | bytes 524304 | tf_op jit(solution)/shard_map/while/body/eval_jaxpr/reduce_scatter | solution.py:103
  725.2 23.1 %all-gather.19.cloned.1.call-done = bf16[1024,1024]{1,0:T(8,128)(2,1)} async-done(((bf16[128,1024]{1,0:T(8,128)(2,1)}), bf16[1024,1024]{1,0:T(8,128)(2,1)}) %all-gather.19.cloned.1.call-update) | async-done | bytes 2097168 | tf_op jit(solution)/shard_map/while/body/eval_jaxpr/all_gather | solution.py:94
  748.3 47.1 %all-gather.17.cloned.1.call-done = bf16[1024,1024]{1,0:T(8,128)(2,1)} async-done(((bf16[256,1024]{1,0:T(8,128)(2,1)}), bf16[1024,1024]{1,0:T(8,128)(2,1)}) %all-gather.17.cloned.1.call-update) | async-done | bytes 2097168 | tf_op jit(solution)/shard_map/while/body/eval_jaxpr/all_gather | solution.py:100
  810.8 31.1 %all-gather.23.cloned.1.call-done = bf16[1,1024,1024]{2,1,0:T(8,128)(2,1)} async-done(((bf16[1,256,1024]{2,1,0:T(8,128)(2,1)}), bf16[1,1024,1024]{2,1,0:T(8,128)(2,1)}) %all-gather.23.cloned.1.call-update) | async-done | bytes 2097168 | tf_op jit(solution)/shard_map/while/body/eval_jaxpr/all_gather | solution.py:108
  841.9 28.9 %all-gather.21.cloned.1.call-done = bf16[1024,1024]{1,0:T(8,128)(2,1)} async-done(((bf16[128,1024]{1,0:T(8,128)(2,1)}), bf16[1024,1024]{1,0:T(8,128)(2,1)}) %all-gather.21.cloned.1.call-update) | async-done | bytes 2097168 | tf_op jit(solution)/shard_map/while/body/eval_jaxpr/all_gather | solution.py:95
  884.3 42.9 %reduce-scatter.19.cloned.1.call-done = bf16[256,1024]{1,0:T(8,128)(2,1)} async-done(((bf16[1024,1024]{1,0:T(8,128)(2,1)}), bf16[256,1024]{1,0:T(8,128)(2,1)}) %reduce-scatter.19.cloned.1.call-update) | async-done | bytes 524304 | tf_op jit(solution)/shard_map/while/body/eval_jaxpr/reduce_scatter | solution.py:111
  942.1 37.1 %all-gather.25.cloned.1.call-done = bf16[1024,1024]{1,0:T(8,128)(2,1)} async-done(((bf16[256,1024]{1,0:T(8,128)(2,1)}), bf16[1024,1024]{1,0:T(8,128)(2,1)}) %all-gather.25.cloned.1.call-update) | async-done | bytes 2097168 | tf_op jit(solution)/shard_map/while/body/eval_jaxpr/all_gather | solution.py:108
  1078.0 16.8 %reduce-scatter.21.cloned.1.call-done = bf16[256,1024]{1,0:T(8,128)(2,1)} async-done(((bf16[1024,1024]{1,0:T(8,128)(2,1)}), bf16[256,1024]{1,0:T(8,128)(2,1)}) %reduce-scatter.21.cloned.1.call-update) | async-done | bytes 524304 | tf_op jit(solution)/shard_map/while/body/eval_jaxpr/reduce_scatter | solution.py:111
  1117.5 40.5 %all-reduce = (f32[1024]{0:T(1024)}, f32[1024]{0:T(1024)}, f32[3072]{0:T(1024)S(1)}, f32[1024]{0:T(1024)}, f32[1024]{0:T(1024)}, /*index=5*/f32[1024]{0:T(1024)}, f32[4096]{0:T(1024)S(1)}, f32[1024]{0:T(1024)}) all-reduce(f32[1024]{0:T(1024)S(1)} %copy-done.58, ...), channel_id=1, replica_groups=mesh['dp'=8,'tensor'=4] {'dp','tensor'}, use_global_device_ids=true, to_apply=%region_28.29 | all-reduce | flops 13312 | bytes 106496 | tf_op jit(solution)/shard_map/psum | solution.py:326
  1160.8 21.7 %reduce-scatter.9.cloned.1.call-done = bf16[128,768]{1,0:T(8,128)(2,1)} async-done(((bf16[1024,768]{1,0:T(8,128)(2,1)}), bf16[128,768]{1,0:T(8,128)(2,1)}) %reduce-scatter.9.cloned.1.call-update) | async-done | bytes 196624 | tf_op jit(solution)/shard_map/reduce_scatter | solution.py:304
  1184.2 42.5 %reduce-scatter.13.cloned.1.call-done = bf16[128,1024]{1,0:T(8,128)(2,1)} async-done(((bf16[1024,1024]{1,0:T(8,128)(2,1)}), bf16[128,1024]{1,0:T(8,128)(2,1)}) %reduce-scatter.13.cloned.1.call-update) | async-done | bytes 262160 | tf_op jit(solution)/shard_map/reduce_scatter | solution.py:310
  1228.5 42.5 %reduce-scatter.15.cloned.1.call-done = bf16[128,1024]{1,0:T(8,128)(2,1)} async-done(((bf16[1024,1024]{1,0:T(8,128)(2,1)}), bf16[128,1024]{1,0:T(8,128)(2,1)}) %reduce-scatter.15.cloned.1.call-update) | async-done | bytes 262160 | tf_op jit(solution)/shard_map/reduce_scatter | solution.py:313
  (565 shorter events, 458.2 us)
Async XLA Ops:
  13.0 78.6 %all-gather.13.cloned.1.call-start = ((), (), s32[]{:S(2)}) async-start(), calls=%async_computation.12 | async-start | bytes 2621440 | tf_op jit(solution)/shard_map/while/body/eval_jaxpr/all_gather | solution.py:100
  17.8 157.9 %reduce-scatter.17.cloned.1.call-start = ((), (), s32[]{:S(2)}) async-start(), calls=%async_computation.14 | async-start | bytes 2621440 | tf_op jit(solution)/shard_map/while/body/eval_jaxpr/reduce_scatter | solution.py:103
  133.4 71.9 %all-gather.19.cloned.1.call-start = ((), (), s32[]{:S(2)}) async-start(), calls=%async_computation.16 | async-start | bytes 2359296 | tf_op jit(solution)/shard_map/while/body/eval_jaxpr/all_gather | solution.py:94
  134.0 118.4 %all-gather.17.cloned.1.call-start = ((), (), s32[]{:S(2)}) async-start(), calls=%async_computation.15 | async-start | bytes 2621440 | tf_op jit(solution)/shard_map/while/body/eval_jaxpr/all_gather | solution.py:100
  180.7 118.3 %all-gather.23.cloned.1.call-start = ((), (), s32[]{:S(2)}) async-start(), calls=%async_computation.18 | async-start | bytes 2621440 | tf_op jit(solution)/shard_map/while/body/eval_jaxpr/all_gather | solution.py:108
  181.6 146.4 %all-gather.21.cloned.1.call-start = ((), (), s32[]{:S(2)}) async-start(), calls=%async_computation.17 | async-start | bytes 2359296 | tf_op jit(solution)/shard_map/while/body/eval_jaxpr/all_gather | solution.py:95
  182.4 202.1 %reduce-scatter.19.cloned.1.call-start = ((), (), s32[]{:S(2)}) async-start(), calls=%async_computation.19 | async-start | bytes 2621440 | tf_op jit(solution)/shard_map/while/body/eval_jaxpr/reduce_scatter | solution.py:111
  341.5 95.0 %all-gather.25.cloned.1.call-start = ((), (), s32[]{:S(2)}) async-start(), calls=%async_computation.20 | async-start | bytes 2621440 | tf_op jit(solution)/shard_map/while/body/eval_jaxpr/all_gather | solution.py:108
  391.2 129.4 %reduce-scatter.23.cloned.1.call-start = ((), (), s32[]{:S(2)}) async-start(), calls=%async_computation.22 | async-start | bytes 2621440 | tf_op jit(solution)/shard_map/while/body/eval_jaxpr/reduce_scatter | solution.py:103
  399.1 153.0 %reduce-scatter.21.cloned.1.call-start = ((), (), s32[]{:S(2)}) async-start(), calls=%async_computation.21 | async-start | bytes 2621440 | tf_op jit(solution)/shard_map/while/body/eval_jaxpr/reduce_scatter | solution.py:111
  558.6 76.0 %all-gather.13.cloned.1.call-start = ((), (), s32[]{:S(2)}) async-start(), calls=%async_computation.12 | async-start | bytes 2621440 | tf_op jit(solution)/shard_map/while/body/eval_jaxpr/all_gather | solution.py:100
  563.4 155.3 %reduce-scatter.17.cloned.1.call-start = ((), (), s32[]{:S(2)}) async-start(), calls=%async_computation.14 | async-start | bytes 2621440 | tf_op jit(solution)/shard_map/while/body/eval_jaxpr/reduce_scatter | solution.py:103
  676.4 71.9 %all-gather.19.cloned.1.call-start = ((), (), s32[]{:S(2)}) async-start(), calls=%async_computation.16 | async-start | bytes 2359296 | tf_op jit(solution)/shard_map/while/body/eval_jaxpr/all_gather | solution.py:94
  676.9 118.4 %all-gather.17.cloned.1.call-start = ((), (), s32[]{:S(2)}) async-start(), calls=%async_computation.15 | async-start | bytes 2621440 | tf_op jit(solution)/shard_map/while/body/eval_jaxpr/all_gather | solution.py:100
  723.6 118.2 %all-gather.23.cloned.1.call-start = ((), (), s32[]{:S(2)}) async-start(), calls=%async_computation.18 | async-start | bytes 2621440 | tf_op jit(solution)/shard_map/while/body/eval_jaxpr/all_gather | solution.py:108
  724.6 146.2 %all-gather.21.cloned.1.call-start = ((), (), s32[]{:S(2)}) async-start(), calls=%async_computation.17 | async-start | bytes 2359296 | tf_op jit(solution)/shard_map/while/body/eval_jaxpr/all_gather | solution.py:95
  725.2 202.1 %reduce-scatter.19.cloned.1.call-start = ((), (), s32[]{:S(2)}) async-start(), calls=%async_computation.19 | async-start | bytes 2621440 | tf_op jit(solution)/shard_map/while/body/eval_jaxpr/reduce_scatter | solution.py:111
  884.3 95.0 %all-gather.25.cloned.1.call-start = ((), (), s32[]{:S(2)}) async-start(), calls=%async_computation.20 | async-start | bytes 2621440 | tf_op jit(solution)/shard_map/while/body/eval_jaxpr/all_gather | solution.py:108
  934.0 132.9 %reduce-scatter.23.cloned.1.call-start = ((), (), s32[]{:S(2)}) async-start(), calls=%async_computation.22 | async-start | bytes 2621440 | tf_op jit(solution)/shard_map/while/body/eval_jaxpr/reduce_scatter | solution.py:103
  941.9 153.0 %reduce-scatter.21.cloned.1.call-start = ((), (), s32[]{:S(2)}) async-start(), calls=%async_computation.21 | async-start | bytes 2621440 | tf_op jit(solution)/shard_map/while/body/eval_jaxpr/reduce_scatter | solution.py:111
  1103.4 55.9 %reduce-scatter.11.cloned.1.call-start = ((), (), s32[]{:S(2)}) async-start(), calls=%async_computation.9 | async-start | bytes 589824 | tf_op jit(solution)/shard_map/reduce_scatter | solution.py:307
  1105.6 77.0 %reduce-scatter.9.cloned.1.call-start = ((), (), s32[]{:S(2)}) async-start(), calls=%async_computation.8 | async-start | bytes 1769472 | tf_op jit(solution)/shard_map/reduce_scatter | solution.py:304
  1108.8 117.9 %reduce-scatter.13.cloned.1.call-start = ((), (), s32[]{:S(2)}) async-start(), calls=%async_computation.10 | async-start | bytes 2359296 | tf_op jit(solution)/shard_map/reduce_scatter | solution.py:310
  1112.8 158.2 %reduce-scatter.15.cloned.1.call-start = ((), (), s32[]{:S(2)}) async-start(), calls=%async_computation.11 | async-start | bytes 2359296 | tf_op jit(solution)/shard_map/reduce_scatter | solution.py:313
  (146 other events, 3093.8 us)
Sparse Core Ops, SparseCore 0:
  15.0 29.3 all-gather.14
  46.5 45.0 all-gather.12
  133.5 42.1 reduce-scatter.16
  177.5 27.7 all-gather.18
  207.3 45.0 all-gather.16
  254.4 44.4 all-gather.22
  300.8 27.1 all-gather.20
  341.6 42.8 reduce-scatter.18
  391.3 45.0 all-gather.24
  438.6 42.1 reduce-scatter.22
  509.8 42.1 reduce-scatter.20
  560.4 26.8 all-gather.14
  589.5 45.0 all-gather.12
  676.5 42.1 reduce-scatter.16
  720.5 27.7 all-gather.18
  750.3 45.0 all-gather.16
  797.4 44.4 all-gather.22
  843.6 27.1 all-gather.20
  884.4 42.8 reduce-scatter.18
  934.1 45.0 all-gather.24
  981.5 42.1 reduce-scatter.22
  1052.6 42.1 reduce-scatter.20
Sparse Core Ops, SparseCore 1:
  1107.6 33.3 reduce-scatter.10
  1144.1 38.4 reduce-scatter.8
  1185.7 41.0 reduce-scatter.12
  1230.0 41.0 reduce-scatter.14
where the time goes:
time: 1290 us; the launch traced here: 1280 us
  waiting for transfers between devices  772 us (60%)
  matrix products  199 us (15%)
  other arithmetic  115 us (9%)
  local copies, waits for them, and re-layouts  104 us (8%)
  blocking collectives  67.7 us (5%)
  between operations  16.3 us (1%)
    all_gather x4, waiting for transfers between devices, seq_gather(): return lax.all_gather(values, 'tensor', axis=0, tiled=True)  189 us
    all_gather x4, waiting for transfers between devices, grad_gather(): return lax.all_gather(values, 'tensor', axis=0, tiled=True)  136 us
    reduce_scatter x4, waiting for transfers between devices, grad_sum(): lax.psum_scatter(values.astype(jnp.bfloat16), 'tensor', scatter_dimension...  125 us
    reduce_scatter x4, waiting for transfers between devices, part_sum(): lax.psum_scatter(values.astype(jnp.bfloat16), 'tensor', scatter_dimension...  83.5 us
    dot_general x16, matrix products, contract(): lax.dot_general(left, right, (((left_dim,), (right_dim,)), ((), ())), pre...  69.9 us
    all_gather x2, waiting for transfers between devices, fetch(): lax.all_gather(fc2_weight, 'dp', axis=0, tiled=True)  58 us
    all_gather x2, waiting for transfers between devices, fetch(): lax.all_gather(fc1_weight, 'dp', axis=0, tiled=True)  45.9 us
    reduce_scatter x1, waiting for transfers between devices, body(): lax.psum_scatter(totals[10].astype(jnp.bfloat16), 'dp', scatter_dimension...  42.5 us
  transfers between devices with their start and end apart: 26, of which 23 were waited for; matrix products, arithmetic and copies ran while one was open for 21% of the time, Pallas kernels for 0%

commit v1 on v0

--- a/solution.py
+++ b/solution.py
@@ -347,6 +347,306 @@
     )
 
 
+SWAP_CORE, SWAP_X, SWAP_Y = 1, 2, 4
+
+
+def one_clip_per_chip(mesh):
+    return mesh.shape["dp"] == 8 and mesh.shape["tensor"] == 4
+
+
+def swap(values, bit):
+    return lax.ppermute(values, "dp", [(i, i ^ bit) for i in range(8)])
+
+
+def shift(values, step):
+    return lax.ppermute(values, "tensor", [(i, (i + step) % 4) for i in range(4)])
+
+
+def clip_routes(back):
+    routes = []
+    for turn in range(2):
+        pairs = []
+        for column in range(4):
+            for core in range(2):
+                for place in range(4):
+                    source = (2 * column + core) * 4 + place
+                    target = (2 * column + place // 2) * 4 + 2 * core + (turn ^ (place % 2))
+                    pairs.append((target, source) if back else (source, target))
+        routes.append(pairs)
+    return routes
+
+
+def pick(flag, first, second):
+    return jnp.where(flag, second, first)
+
+
+def to_clips(values):
+    odd = lax.axis_index("tensor") % 2 == 1
+    arrived = []
+    for turn, pairs in enumerate(clip_routes(False)):
+        sent = pick(odd, values[turn], values[1 - turn])
+        arrived.append(lax.ppermute(sent, ("dp", "tensor"), pairs))
+    return jnp.concatenate(
+        [pick(odd, arrived[0], arrived[1]), pick(odd, arrived[1], arrived[0])], axis=0
+    )
+
+
+def from_clips(values):
+    odd = lax.axis_index("tensor") % 2 == 1
+    rows = values.shape[0] // 2
+    arrived = []
+    for turn, pairs in enumerate(clip_routes(True)):
+        sent = pick(odd, values[turn * rows : (turn + 1) * rows], values[(1 - turn) * rows : (2 - turn) * rows])
+        arrived.append(lax.ppermute(sent, ("dp", "tensor"), pairs))
+    return jnp.stack([pick(odd, arrived[0], arrived[1]), pick(odd, arrived[1], arrived[0])])
+
+
+def three_parts(values):
+    high = lax.reduce_precision(values, 8, 7)
+    rest = values - high
+    middle = lax.reduce_precision(rest, 8, 7)
+    low = rest - middle
+    return jnp.stack([high, middle, low]).astype(jnp.bfloat16)
+
+
+def clip_body(
+    activations,
+    cotangent,
+    attn_gain,
+    attn_shift,
+    qkv_weight,
+    qkv_bias,
+    out_weight,
+    out_bias,
+    mlp_gain,
+    mlp_shift,
+    fc1_weight,
+    fc1_bias,
+    fc2_weight,
+    fc2_bias,
+):
+    index = lax.axis_index("dp")
+    core = index % 2
+    at_x = index // 2 % 2
+    at_y = index // 4
+    width = activations.shape[2]
+    length = activations.shape[1] * 4
+    half_rows = length // 2
+    own_rows = qkv_weight.shape[0]
+    heads_here = qkv_weight.shape[1] // (3 * HD)
+    half_heads = heads_here // 2
+    heads = 4 * half_heads
+    qkv_cols = half_heads * 3 * HD
+    out_cols = out_weight.shape[1] // 2
+    unit_cols = fc1_weight.shape[1] // 2
+    factor = 1.0 / math.sqrt(HD)
+    low = jnp.bfloat16
+
+    def first_half(values):
+        return lax.slice_in_dim(values, 0, values.shape[-1] // 2, axis=values.ndim - 1)
+
+    def second_half(values):
+        return lax.slice_in_dim(values, values.shape[-1] // 2, values.shape[-1], axis=values.ndim - 1)
+
+    def own_half(values):
+        return pick(core == 1, first_half(values), second_half(values))
+
+    def other_half(values):
+        return pick(core == 1, second_half(values), first_half(values))
+
+    def by_kind(values):
+        lead = values.shape[:-1]
+        split = values.reshape(lead + (2, half_heads, 3, HD))
+        return jnp.swapaxes(split, -3, -2).reshape(values.shape)
+
+    def by_head(values):
+        lead = values.shape[:-1]
+        split = values.reshape(lead + (2, 3, half_heads, HD))
+        return jnp.swapaxes(split, -3, -2).reshape(values.shape)
+
+    tokens = to_clips(activations).astype(jnp.float32)
+
+    columns = (by_kind(qkv_weight), out_weight, fc1_weight, fc2_weight)
+    biases = (by_kind(qkv_bias), None, fc1_bias, None)
+    mine = jnp.concatenate([own_half(item) for item in columns], axis=1)
+    theirs = swap(jnp.concatenate([other_half(item) for item in columns], axis=1), SWAP_CORE)
+    rows = jnp.stack([pick(core == 1, mine, theirs), pick(core == 1, theirs, mine)])
+
+    def along_z(values):
+        return jnp.stack([values] + [shift(values, step) for step in (1, 2, 3)], axis=values.ndim - 1)
+
+    def over_plane(values):
+        even, odd = values[0], values[1]
+        even_x = swap(even, SWAP_X)
+        odd_y = swap(odd, SWAP_Y)
+        even = jnp.stack([pick(at_x == 1, even, even_x), pick(at_x == 1, even_x, even)])
+        odd = jnp.stack([pick(at_y == 1, odd, odd_y), pick(at_y == 1, odd_y, odd)])
+        even_y = swap(even, SWAP_Y)
+        odd_x = swap(odd, SWAP_X)
+        even = jnp.stack([pick(at_y == 1, even, even_y), pick(at_y == 1, even_y, even)])
+        odd = jnp.stack([pick(at_x == 1, odd, odd_x), pick(at_x == 1, odd_x, odd)], axis=1)
+        whole = jnp.stack([even, odd], axis=2)
+        return whole.reshape((4 * 2 * own_rows, -1))
+
+    bounds = [0, qkv_cols, qkv_cols + out_cols, qkv_cols + out_cols + unit_cols, qkv_cols + out_cols + 2 * unit_cols]
+
+    def widened(part, bias):
+        lines = jnp.zeros((16, part.shape[-1]), low)
+        lines = lines.at[:3].set(three_parts(own_half(bias)))
+        return jnp.concatenate([part.reshape(-1, part.shape[-1]), lines], axis=0)
+
+    def parted(values, cols):
+        body_rows, lines = values[: 2 * own_rows], values[2 * own_rows :]
+        bias = jnp.sum(lines[:3].astype(jnp.float32), axis=0).reshape(-1)
+        return body_rows.reshape(2, own_rows, 4, cols), bias
+
+    qkv_z, bias_qkv = parted(along_z(widened(rows[:, :, : bounds[1]], biases[0])), qkv_cols)
+    weight_qkv = over_plane(qkv_z)
+    out_z = along_z(rows[:, :, bounds[1] : bounds[2]])
+    weight_out = over_plane(out_z)
+    up_z, bias_up = parted(along_z(widened(rows[:, :, bounds[2] : bounds[3]], biases[2])), unit_cols)
+    weight_up = over_plane(up_z)
+    down_z = along_z(rows[:, :, bounds[3] :])
+    weight_down = over_plane(down_z)
+
+    def both_halves(values):
+        other = swap(values, SWAP_CORE)
+        return jnp.concatenate([pick(core == 1, values, other), pick(core == 1, other, values)], axis=0)
+
+    def part_sum(values):
+        halves = values.reshape((2, half_rows) + values.shape[1:])
+        sent = pick(core == 1, halves[1], halves[0]).astype(low)
+        return pick(core == 1, halves[0], halves[1]) + swap(sent, SWAP_CORE).astype(jnp.float32)
+
+    cosine, sine = rotary_tables(length)
+    cosine = cosine[:, None, :]
+    sine = sine[:, None, :]
+
+    def rotate(values):
+        return values * cosine + pair_swap(values) * sine
+
+    def rotate_back(values):
+        return values * cosine + pair_swap(values * sine)
+
+    first_all = both_halves(norm_rows(tokens, attn_gain, attn_shift).astype(low))
+    packed = jnp.dot(first_all, weight_qkv, preferred_element_type=jnp.float32) + bias_qkv
+    packed = packed.reshape(length, 4, 3, half_heads, HD)
+    query = rotate(packed[:, :, 0].reshape(length, heads, HD)).astype(low)
+    key = rotate(packed[:, :, 1].reshape(length, heads, HD)).astype(low)
+    value = packed[:, :, 2].reshape(length, heads, HD).astype(low)
+    scores = jnp.einsum("qhd,khd->hqk", query, key, preferred_element_type=jnp.float32) * factor
+    row_max = jnp.max(scores, axis=-1, keepdims=True)
+    expo = jnp.exp(scores - row_max)
+    row_total = jnp.sum(expo, axis=-1, keepdims=True)
+    weights_low = (expo / row_total).astype(low)
+    heads_out = jnp.einsum("hqk,khd->qhd", weights_low, value, preferred_element_type=jnp.float32)
+    heads_out = heads_out.reshape(length, heads * HD).astype(low)
+    log_total = row_max + jnp.log(row_total)
+    resid = tokens + part_sum(contract(heads_out, weight_out, 1, 1)) + out_bias
+    second_all = both_halves(norm_rows(resid, mlp_gain, mlp_shift).astype(low))
+    hidden = jnp.dot(second_all, weight_up, preferred_element_type=jnp.float32) + bias_up
+    act = exact_gelu(hidden).astype(low)
+    result = resid + part_sum(contract(act, weight_down, 1, 1)) + fc2_bias
+    output = from_clips(result.astype(low))
+
+    def to_owner(grad, cols):
+        parts = grad.astype(low).reshape(2, 2, 2, own_rows, 4 * cols)
+        even, odd = parts[:, :, 0], parts[:, :, 1]
+        even = pick(at_y == 1, even[0], even[1]) + swap(pick(at_y == 1, even[1], even[0]), SWAP_Y)
+        odd = pick(at_x == 1, odd[:, 0], odd[:, 1]) + swap(pick(at_x == 1, odd[:, 1], odd[:, 0]), SWAP_X)
+        even = pick(at_x == 1, even[0], even[1]) + swap(pick(at_x == 1, even[1], even[0]), SWAP_X)
+        odd = pick(at_y == 1, odd[0], odd[1]) + swap(pick(at_y == 1, odd[1], odd[0]), SWAP_Y)
+        both = jnp.stack([even, odd]).reshape(2, own_rows, 4, cols)
+        total = both[:, :, 0].astype(jnp.float32)
+        for step in (1, 2, 3):
+            total = total + shift(both[:, :, step], 4 - step).astype(jnp.float32)
+        total = total.astype(low)
+        kept = pick(core == 1, total[0], total[1])
+        came = swap(pick(core == 1, total[1], total[0]), SWAP_CORE)
+        return jnp.concatenate(
+            [pick(core == 1, kept, came), pick(core == 1, came, kept)], axis=-1
+        ).astype(jnp.float32)
+
+    grad_own = to_clips(cotangent)
+    grad_top = grad_own.astype(jnp.float32)
+    grad_all = both_halves(grad_own)
+    sum_fc2_bias = jnp.sum(grad_top, axis=0)
+    grad_fc2_weight = to_owner(contract(grad_all, act, 0, 0), unit_cols)
+    grad_act = jnp.dot(grad_all, weight_down, preferred_element_type=jnp.float32)
+    grad_hidden = jax.vjp(exact_gelu, hidden)[1](grad_act)[0].astype(low)
+    sum_fc1_bias = jnp.sum(grad_hidden, axis=0, dtype=jnp.float32)
+    grad_fc1_weight = to_owner(contract(second_all, grad_hidden, 0, 0), unit_cols)
+    grad_second = part_sum(contract(grad_hidden, weight_up, 1, 1))
+    second_pull = jax.vjp(norm_rows, resid, mlp_gain, mlp_shift)[1]
+    grad_resid_norm, sum_mlp_gain, sum_mlp_shift = second_pull(grad_second)
+    grad_resid = grad_top + grad_resid_norm
+    sum_out_bias = jnp.sum(grad_resid, axis=0)
+    resid_all = both_halves(grad_resid.astype(low))
+    grad_out_weight = to_owner(contract(resid_all, heads_out, 0, 0), out_cols)
+    grad_heads = jnp.dot(resid_all, weight_out, preferred_element_type=jnp.float32).astype(low)
+    grad_heads = grad_heads.reshape(length, heads, HD)
+    scores = jnp.einsum("qhd,khd->hqk", query, key, preferred_element_type=jnp.float32) * factor
+    probs = jnp.exp(scores - log_total)
+    grad_value = jnp.einsum(
+        "hqk,qhd->khd", probs.astype(low), grad_heads, preferred_element_type=jnp.float32
+    )
+    grad_probs = jnp.einsum("qhd,khd->hqk", grad_heads, value, preferred_element_type=jnp.float32)
+    grad_scores = (
+        probs * (grad_probs - jnp.sum(probs * grad_probs, axis=-1, keepdims=True))
+    ).astype(low)
+    grad_query = factor * jnp.einsum("hqk,khd->qhd", grad_scores, key, preferred_element_type=jnp.float32)
+    grad_key = factor * jnp.einsum("hqk,qhd->khd", grad_scores, query, preferred_element_type=jnp.float32)
+    kinds = [
+        item.reshape(length, 4, 1, half_heads, HD)
+        for item in (rotate_back(grad_query), rotate_back(grad_key), grad_value)
+    ]
+    grad_packed = jnp.concatenate(kinds, axis=2).reshape(length, 4 * qkv_cols).astype(low)
+    sum_qkv_bias = jnp.sum(grad_packed, axis=0, dtype=jnp.float32)
+    grad_qkv_weight = by_head(to_owner(contract(first_all, grad_packed, 0, 0), qkv_cols))
+    grad_first = part_sum(contract(grad_packed, weight_qkv, 1, 1))
+    first_pull = jax.vjp(norm_rows, tokens, attn_gain, attn_shift)[1]
+    grad_input_norm, sum_attn_gain, sum_attn_shift = first_pull(grad_first)
+    input_grad = from_clips((grad_resid + grad_input_norm).astype(low)).astype(jnp.float32)
+
+    def plane_total(values):
+        values = values + swap(values, SWAP_X)
+        return values + swap(values, SWAP_Y)
+
+    def whole_total(values):
+        values = plane_total(values)
+        values = values + swap(values, SWAP_CORE)
+        for bit in (1, 2):
+            values = values + lax.ppermute(values, "tensor", [(i, i ^ bit) for i in range(4)])
+        return values
+
+    def bias_total(values, cols):
+        blocks = plane_total(values).reshape(4, cols)
+        total = blocks[0]
+        for step in (1, 2, 3):
+            total = total + shift(blocks[step], 4 - step)
+        other = swap(total, SWAP_CORE)
+        return jnp.concatenate([pick(core == 1, total, other), pick(core == 1, other, total)])
+
+    early = whole_total(jnp.stack([sum_fc2_bias, sum_mlp_gain, sum_mlp_shift, sum_out_bias]))
+    late = whole_total(jnp.stack([sum_attn_gain, sum_attn_shift]))
+    return (
+        output,
+        input_grad,
+        late[0],
+        late[1],
+        grad_qkv_weight,
+        by_head(bias_total(sum_qkv_bias, qkv_cols)),
+        grad_out_weight,
+        early[3],
+        early[1],
+        early[2],
+        grad_fc1_weight,
+        bias_total(sum_fc1_bias, unit_cols),
+        grad_fc2_weight,
+        early[0],
+    )
+
+
 def solution(mesh):
     in_specs = (
         P("dp", "tensor", None),
@@ -380,4 +680,5 @@
         P("dp", "tensor"),
         P(),
     )
-    return jax.shard_map(body, mesh=mesh, in_specs=in_specs, out_specs=out_specs, check_vma=False)
+    plan = clip_body if one_clip_per_chip(mesh) else body
+    return jax.shard_map(plan, mesh=mesh, in_specs=in_specs, out_specs=out_specs, check_vma=False)

time: 1290 us -> 849 us (0.66)
  waiting for transfers between devices: 772 us -> 227 us
  starting transfers between devices: 1.42 us -> 138 us
  blocking collectives: 67.7 us -> 0 us
  local copies, waits for them, and re-layouts: 104 us -> 154 us
  other arithmetic: 115 us -> 150 us
  matrix products: 199 us -> 169 us
  between operations: 16.3 us -> 3.01 us
    all_gather x14 -> x0, waiting for transfers between devices: 452 us -> none  [the longest x4 189 us: seq_gather(): return lax.all_gather(values, 'tensor', axis=0, tiled=True)]
    reduce_scatter x12 -> x0, waiting for transfers between devices: 315 us -> none  [the longest x4 125 us: grad_sum(): lax.psum_scatter(values.astype(jnp.bfloat16), 'tensor', scatter_dimension...]
    ppermute x0 -> x99, waiting for transfers between devices: none -> 227 us  [the longest x57 98.7 us: swap(): return lax.ppermute(values, 'dp', [(i, i ^ bit) for i in range(8)])]
    ppermute x0 -> x99, starting transfers between devices: none -> 138 us  [the longest x57 59.1 us: swap(): return lax.ppermute(values, 'dp', [(i, i ^ bit) for i in range(8)])]
    psum x1 -> x0, blocking collectives: 40.5 us -> none  [body(): lax.psum((totals[0], totals[1], qkv_place, totals[5], totals[6], totals[7...]
    dot_general x16 -> x8, matrix products: 69.9 us -> 35.7 us  [contract(): lax.dot_general(left, right, (((left_dim,), (right_dim,)), ((), ())), pre...]
    unnamed x12 -> x202, local copies, waits for them, and re-layouts: 0.04 us -> 30.7 us
    all_gather x2 -> x0, blocking collectives: 27.1 us -> none  [fetch(): lax.all_gather(out_weight, 'dp', axis=0, tiled=True)]
  transfers between devices with their start and end apart: 26 -> 99, of which waited for: 23 -> 38; matrix products, arithmetic and copies ran while one was open for 21% -> 30% of each run, Pallas kernels for 0% -> 0%
where the time goes in v1:
time: 849 us; the launch traced here: 841 us
  waiting for transfers between devices  227 us (27%)
  matrix products  169 us (20%)
  local copies, waits for them, and re-layouts  154 us (18%)
  other arithmetic  150 us (18%)
  starting transfers between devices  138 us (16%)
    ppermute x57, waiting for transfers between devices, swap(): return lax.ppermute(values, 'dp', [(i, i ^ bit) for i in range(8)])  98.7 us
    ppermute x30, waiting for transfers between devices, shift(): lax.ppermute(values, 'tensor', [(i, (i + step) % 4) for i in range(4)])  85.2 us
    ppermute x57, starting transfers between devices, swap(): return lax.ppermute(values, 'dp', [(i, i ^ bit) for i in range(8)])  59.1 us
    rev x4, local copies, waits for them, and re-layouts, pair_swap(): return paired[..., ::-1].reshape(shape)  44.2 us
    dot_general x8, matrix products, contract(): lax.dot_general(left, right, (((left_dim,), (right_dim,)), ((), ())), pre...  35.7 us
    ppermute x30, starting transfers between devices, shift(): lax.ppermute(values, 'tensor', [(i, (i + step) % 4) for i in range(4)])  35.5 us
    unnamed x202, local copies, waits for them, and re-layouts  30.7 us
    convert_element_type x1, other arithmetic, clip_body(): grad_scores = (probs * (grad_probs - jnp.sum(probs * grad_probs, axis=-1,...  28.2 us
  transfers between devices with their start and end apart: 99, of which 38 were waited for; matrix products, arithmetic and copies ran while one was open for 30% of the time, Pallas kernels for 0%

profile of v1, /device:TPU:1, one launch (start us, length us, event | category | flops | bytes accessed | tf_op | source)
XLA Modules:
  0.0 841.2 jit_solution(16216626426934385612)
XLA Ops:
  34.5 12.9 %collective-permute-start.38 = (bf16[256,1024]{1,0:T(8,128)(2,1)S(1)}, bf16[256,1024]{1,0:T(8,128)(2,1)S(1)}, u32[]{:S(2)}, u32[]{:S(2)}) collective-permute-start(bf16[256,1024]{1,0:T(8,128)(2,1)S(1)} %get-tuple-element.152), channel_id=1, source_target_pairs={{0,0},{1,1},{2,4},{3,5},{4,2},{5,3},{6,6},{7,7},{8,8},{9,9},{10,12... | collective-permute-start | bytes 1572872 | tf_op jit(solution)/shard_map/ppermute | solution.py:388
  54.6 22.5 %collective-permute-done.38 = bf16[256,1024]{1,0:T(8,128)(2,1)S(1)} collective-permute-done((bf16[256,1024]{1,0:T(8,128)(2,1)S(1)}, bf16[256,1024]{1,0:T(8,128)(2,1)S(1)}, u32[]{:S(2)}, u32[]{:S(2)}) %collective-permute-start.38) | collective-permute-done | bytes 524320 | tf_op jit(solution)/shard_map/ppermute | solution.py:388
  86.3 14.1 %collective-permute-done.28 = bf16[2,128,512]{2,1,0:T(8,128)(2,1)} collective-permute-done((bf16[2,128,512]{2,1,0:T(8,128)(2,1)}, bf16[2,128,512]{2,1,0:T(8,128)(2,1)}, u32[]{:S(2)}, u32[]{:S(2)}) %collective-permute-start.28) | collective-permute-done | bytes 262176 | tf_op jit(solution)/shard_map/ppermute | solution.py:362
  103.8 18.5 %collective-permute-done.21 = bf16[272,512]{1,0:T(8,128)(2,1)S(1)} collective-permute-done((bf16[272,512]{1,0:T(8,128)(2,1)}, bf16[272,512]{1,0:T(8,128)(2,1)S(1)}, u32[]{:S(2)}, u32[]{:S(2)}) %collective-permute-start.21) | collective-permute-done | bytes 278560 | tf_op jit(solution)/shard_map/ppermute | solution.py:362
  140.4 9.4 %collective-permute-done.30 = bf16[128,4,512]{2,0,1:T(8,128)(2,1)S(1)} collective-permute-done((bf16[128,4,512]{2,0,1:T(8,128)(2,1)S(1)}, bf16[128,4,512]{2,0,1:T(8,128)(2,1)S(1)}, u32[]{:S(2)}, u32[]{:S(2)}) %collective-permute-start.30) | collective-permute-done | bytes 524320 | tf_op jit(solution)/shard_map/ppermute | solution.py:358
  205.9 11.1 %rev.13 = f32[1024,8,32,2]{0,3,2,1:T(2,128)} reverse(f32[1024,8,32,2]{0,3,2,1:T(2,128)} %reshape_reshape_squeeze.7), dimensions={3} | reverse | bytes 4194304 | tf_op jit(solution)/shard_map/rev | solution.py:40
  224.0 11.0 %rev.12 = f32[1024,8,32,2]{0,3,2,1:T(2,128)} reverse(f32[1024,8,32,2]{0,3,2,1:T(2,128)} %reshape_reshape_squeeze.6), dimensions={3} | reverse | bytes 4194304 | tf_op jit(solution)/shard_map/rev | solution.py:40
  242.7 13.2 %multiply_reduce_fusion.1 = (f32[8,1024]{1,0:T(8,128)S(1)}, f32[8,1024,1024]{1,2,0:T(8,128)}) fusion(bf16[1024,8,64]{0,2,1:T(8,128)(2,1)S(1)} %get-tuple-element.181, bf16[1024,8,64]{0,2,1:T(8,128)(2,1)S(1)} %get-tuple-element.180), kind=kOutput, calls=%fused_computation.6 | convolution fusion | flops 1090510848 | bytes 35684352 | tf_op jit(solution)/shard_map/qhd,khd->hqk/dot_general | solution.py:537
  255.9 13.6 %fusion = f32[8,1024]{1,0:T(8,128)S(1)} fusion(f32[8,1024,1024]{1,2,0:T(8,128)} %get-tuple-element.244, f32[8,1024]{1,0:T(8,128)S(1)} %get-tuple-element.243), kind=kLoop, calls=%fused_computation.5 | loop fusion | flops 25157632 | bytes 33619968 | tf_op jit(solution)/shard_map/reduce_sum | solution.py:540
  269.6 13.5 %fusion.29 = bf16[8,64,1024]{2,1,0:T(8,128)(2,1)S(1)} fusion(bf16[1024,8,64]{0,2,1:T(8,128)(2,1)S(1)} %bitcast.452, f32[8,1024,1024]{1,2,0:T(8,128)} %get-tuple-element.244, f32[8,1024]{1,0:T(8,128)S(1)} %fusion, f32[8,1024]{1,0:T(8,128)S(1)} %get-tuple-element.243), kind=kOutput, calls=%fused_computation.93 | convolution fusion | flops 1107820544 | bytes 35717120 | tf_op jit(solution)/shard_map/hqk,khd->qhd/dot_general | solution.py:542
  313.4 25.4 %multiply_convert_fusion.1 = (bf16[1024,2048]{1,0:T(8,128)(2,1)S(1)}, f32[1024,2048]{1,0:T(8,128)}, f32[1024,2048]{1,0:T(8,128)}) fusion(f32[2048]{0:T(1024)S(1)} %bitcast.527, bf16[1024,2048]{1,0:T(8,128)(2,1)S(1)} %bitcast.460, bf16[512,1024]{1,0:T(8,128)(2,1)S(1)} %get-tuple-element.110, bf16[512,1024]{1,0:T(8,128)(2,1)S(1)} %get-tuple-element.109), kind=kOutput, calls=%fused_computation.14 | convolution fusion | flops 4437573632 | bytes 27271168 | tf_op jit(solution)/shard_map/dot_general | solution.py:547
  350.1 13.3 %convert_reduce_fusion = (f32[2048]{0:T(1024)S(1)}, bf16[1024,2048]{1,0:T(8,128)(2,1)}) fusion(f32[1024,2048]{1,0:T(8,128)} %get-tuple-element.86, bf16[1024,2048]{1,0:T(8,128)(2,1)S(1)} %bitcast.457, bf16[512,1024]{1,0:T(8,128)(2,1)S(1)} %copy-done.60, bf16[512,1024]{1,0:T(8,128)(2,1)S(1)} %copy-done.59, f32[1024,2048]{1,0:T(8,128)} %get-tuple-element.245, ...), kind=kOutput, calls=%fused_computation.12 | convolution fusion | flops 4334811136 | bytes 27279360 | tf_op jit(solution)/shard_map/dot_general | solution.py:575
  448.3 14.9 %collective-permute-done.91 = bf16[2,128,2048]{1,2,0:T(8,128)(2,1)S(1)} collective-permute-done((bf16[2,128,2048]{1,2,0:T(8,128)(2,1)S(1)}, bf16[2,128,2048]{1,2,0:T(8,128)(2,1)S(1)}, u32[]{:S(2)}, u32[]{:S(2)}) %collective-permute-start.91) | collective-permute-done | bytes 1048608 | tf_op jit(solution)/shard_map/ppermute | solution.py:358
  469.6 10.0 %collective-permute-done.73 = f32[4,1024]{1,0:T(4,128)S(1)} collective-permute-done((f32[4,1024]{1,0:T(4,128)S(1)}, f32[4,1024]{1,0:T(4,128)S(1)}, u32[]{:S(2)}, u32[]{:S(2)}) %collective-permute-start.73) | collective-permute-done | bytes 16416 | tf_op jit(solution)/shard_map/ppermute | solution.py:358
  523.4 21.3 %collective-permute-done.82 = bf16[2,128,512]{2,1,0:T(8,128)(2,1)S(1)} collective-permute-done((bf16[2,128,512]{2,1,0:T(8,128)(2,1)S(1)}, bf16[2,128,512]{2,1,0:T(8,128)(2,1)S(1)}, u32[]{:S(2)}, u32[]{:S(2)}) %collective-permute-start.82) | collective-permute-done | bytes 262176 | tf_op jit(solution)/shard_map/ppermute | solution.py:362
  565.4 15.0 %fusion.2 = bf16[8,64,1024]{2,1,0:T(8,128)(2,1)} fusion(bf16[1024,8,64]{0,2,1:T(8,128)(2,1)S(1)} %bitcast.450, f32[8,1024,1024]{1,2,0:T(8,128)} %get-tuple-element.244, f32[8,1024]{1,0:T(8,128)S(1)} %copy-done.54), kind=kOutput, calls=%fused_computation.8 | convolution fusion | flops 1098907648 | bytes 35684352 | tf_op jit(solution)/shard_map/hqk,qhd->khd/dot_general | solution.py:590
  580.4 22.4 %multiply_reduce_fusion = (f32[8,1024]{1,0:T(8,128)S(1)}, f32[8,1024,1024]{1,2,0:T(8,128)}) fusion(f32[8,1024,1024]{1,2,0:T(8,128)} %get-tuple-element.244, f32[8,1024]{1,0:T(8,128)S(1)} %copy-done.54, bf16[1024,8,64]{0,2,1:T(8,128)(2,1)S(1)} %bitcast.451, bf16[1024,8,64]{0,2,1:T(8,128)(2,1)S(1)} %bitcast.453), kind=kOutput, calls=%fused_computation.1 | convolution fusion | flops 1107288064 | bytes 69271552 | tf_op jit(solution)/shard_map/qhd,khd->hqk/dot_general | solution.py:593
  602.8 28.2 %multiply_convert_fusion = bf16[8,1024,1024]{1,2,0:T(8,128)(2,1)} fusion(f32[8,1024,1024]{1,2,0:T(8,128)} %get-tuple-element.247, f32[8,1024,1024]{1,2,0:T(8,128)} %get-tuple-element.244, f32[8,1024]{1,0:T(8,128)S(1)} %get-tuple-element.246, f32[8,1024]{1,0:T(8,128)S(1)} %copy-done.54), kind=kLoop, calls=%fused_computation | loop fusion | flops 41943040 | bytes 83951616 | tf_op jit(solution)/shard_map/convert_element_type | solution.py:596
  631.0 11.4 %fusion.145 = f32[8,64,1024]{2,1,0:T(8,128)S(1)} fusion(bf16[1024,8,64]{0,2,1:T(8,128)(2,1)} %copy-done.18, bf16[8,1024,1024]{1,2,0:T(8,128)(2,1)} %multiply_convert_fusion), kind=kOutput, calls=%fused_computation.444 | convolution fusion | flops 1073741824 | bytes 19922944 | tf_op jit(solution)/shard_map/hqk,qhd->khd/dot_general | solution.py:598
  642.4 11.6 %bitcast_multiply_fusion.2 = (f32[1024,8,64]{0,2,1:T(8,128)}, f32[1024,8,64]{0,2,1:T(8,128)}, f32[8,64,1024]{2,1,0:T(8,128)}) fusion(f32[1024,64]{0,1:T(8,128)S(1)} %copy-done.48, f32[8,64,1024]{2,1,0:T(8,128)S(1)} %fusion.145, bf16[1024,8,64]{0,2,1:T(8,128)(2,1)S(1)} %copy-done.11, bf16[8,1024,1024]{1,2,0:T(8,128)(2,1)} %multiply_convert_fusion), kind=kOutput, calls=%fused_computation.68 | convolution fusion | flops 1074790400 | bytes 26476544 | tf_op jit(solution)/shard_map/hqk,khd->qhd/dot_general | solution.py:597
  658.0 11.0 %rev.14 = f32[1024,8,32,2]{0,3,2,1:T(2,128)} reverse(f32[1024,8,32,2]{0,3,2,1:T(2,128)} %reshape.646), dimensions={3} | reverse | bytes 4194304 | tf_op jit(solution)/shard_map/rev | solution.py:40
  676.1 11.1 %rev.15 = f32[1024,8,32,2]{0,3,2,1:T(2,128)} reverse(f32[1024,8,32,2]{0,3,2,1:T(2,128)} %reshape.649), dimensions={3} | reverse | bytes 4194304 | tf_op jit(solution)/shard_map/rev | solution.py:40
  741.1 10.4 %collective-permute-done.65 = bf16[128,512]{0,1:T(8,128)(2,1)} collective-permute-done((bf16[128,512]{0,1:T(8,128)(2,1)}, bf16[128,512]{0,1:T(8,128)(2,1)}, u32[]{:S(2)}, u32[]{:S(2)}) %collective-permute-start.65) | collective-permute-done | bytes 131104 | tf_op jit(solution)/shard_map/ppermute | solution.py:358
  825.0 14.4 %collective-permute-done.44 = bf16[256,1024]{1,0:T(8,128)(2,1)S(1)} collective-permute-done((bf16[256,1024]{1,0:T(8,128)(2,1)S(1)}, bf16[256,1024]{1,0:T(8,128)(2,1)S(1)}, u32[]{:S(2)}, u32[]{:S(2)}) %collective-permute-start.44) | collective-permute-done | bytes 524320 | tf_op jit(solution)/shard_map/ppermute | solution.py:400
  (639 shorter events, 477.7 us)
Async XLA Ops:
  6.4 41.4 %collective-permute-start = (bf16[256,1024]{1,0:T(8,128)(2,1)}, bf16[256,1024]{1,0:T(8,128)(2,1)S(1)}, u32[]{:S(2)}, u32[]{:S(2)}) collective-permute-start(bf16[256,1024]{1,0:T(8,128)(2,1)} %get-tuple-element.163), channel_id=1, source_target_pairs={{0,1},{1,0},{2,5},{3,4},{4,3},{5,2},{6,7},{7,6},{8,9},{9,8},{10,13... | collective-permute-start | bytes 1572872 | tf_op jit(solution)/shard_map/ppermute | solution.py:388
  11.1 36.7 %collective-permute-start.1 = (bf16[256,1024]{1,0:T(8,128)(2,1)}, bf16[256,1024]{1,0:T(8,128)(2,1)S(1)}, u32[]{:S(2)}, u32[]{:S(2)}) collective-permute-start(bf16[256,1024]{1,0:T(8,128)(2,1)} %get-tuple-element.164), channel_id=1, source_target_pairs={{0,0},{1,1},{2,4},{3,5},{4,2},{5,3},{6,6},{7,7},{8,8},{9,9},{10,12... | collective-permute-start | bytes 1572872 | tf_op jit(solution)/shard_map/ppermute | solution.py:388
  34.5 42.6 %collective-permute-start.38 = (bf16[256,1024]{1,0:T(8,128)(2,1)S(1)}, bf16[256,1024]{1,0:T(8,128)(2,1)S(1)}, u32[]{:S(2)}, u32[]{:S(2)}) collective-permute-start(bf16[256,1024]{1,0:T(8,128)(2,1)S(1)} %get-tuple-element.152), channel_id=1, source_target_pairs={{0,0},{1,1},{2,4},{3,5},{4,2},{5,3},{6,6},{7,7},{8,8},{9,9},{10,12... | collective-permute-start | bytes 1572872 | tf_op jit(solution)/shard_map/ppermute | solution.py:388
  47.8 37.9 %collective-permute-start.4 = (bf16[272,384]{1,0:T(8,128)(2,1)S(1)}, bf16[272,384]{1,0:T(8,128)(2,1)S(1)}, u32[]{:S(2)}, u32[]{:S(2)}) collective-permute-start(bf16[272,384]{1,0:T(8,128)(2,1)S(1)} %get-tuple-element.212), channel_id=1, source_target_pairs={{0,1},{1,2},{2,3},{3,0},{4,5},{5,6},{6,7},{7,4},{8,9},{9,10},{10,1... | collective-permute-start | bytes 626696 | tf_op jit(solution)/shard_map/ppermute | solution.py:362
  47.9 37.8 %collective-permute-start.6 = (bf16[272,384]{1,0:T(8,128)(2,1)S(1)}, bf16[272,384]{1,0:T(8,128)(2,1)S(1)}, u32[]{:S(2)}, u32[]{:S(2)}) collective-permute-start(bf16[272,384]{1,0:T(8,128)(2,1)S(1)} %get-tuple-element.212), channel_id=1, source_target_pairs={{0,3},{1,0},{2,1},{3,2},{4,7},{5,4},{6,5},{7,6},{8,11},{9,8},{10,9... | collective-permute-start | bytes 626696 | tf_op jit(solution)/shard_map/ppermute | solution.py:362
  85.7 36.6 %collective-permute-start.21 = (bf16[272,512]{1,0:T(8,128)(2,1)}, bf16[272,512]{1,0:T(8,128)(2,1)S(1)}, u32[]{:S(2)}, u32[]{:S(2)}) collective-permute-start(bf16[272,512]{1,0:T(8,128)(2,1)} %get-tuple-element.195), channel_id=1, source_target_pairs={{0,2},{1,3},{2,0},{3,1},{4,6},{5,7},{6,4},{7,5},{8,10},{9,11},{10,... | collective-permute-start | bytes 835592 | tf_op jit(solution)/shard_map/ppermute | solution.py:362
  85.7 37.8 %collective-permute-start.20 = (bf16[272,512]{1,0:T(8,128)(2,1)}, bf16[272,512]{1,0:T(8,128)(2,1)S(1)}, u32[]{:S(2)}, u32[]{:S(2)}) collective-permute-start(bf16[272,512]{1,0:T(8,128)(2,1)} %get-tuple-element.195), channel_id=1, source_target_pairs={{0,1},{1,2},{2,3},{3,0},{4,5},{5,6},{6,7},{7,4},{8,9},{9,10},{10,1... | collective-permute-start | bytes 835592 | tf_op jit(solution)/shard_map/ppermute | solution.py:362
  100.7 64.2 %collective-permute-start.39 = (bf16[512,1024]{1,0:T(8,128)(2,1)}, bf16[512,1024]{1,0:T(8,128)(2,1)S(1)}, u32[]{:S(2)}, u32[]{:S(2)}) collective-permute-start(bf16[512,1024]{1,0:T(8,128)(2,1)} %pad_maximum_fusion.26), channel_id=1, source_target_pairs={{0,4},{4,0},{8,12},{12,8},{16,20},{20,16},{24,28},{28,24},{1,5},{5... | collective-permute-start | bytes 3145736 | tf_op jit(solution)/shard_map/ppermute | solution.py:358
  100.8 67.3 %collective-permute-start.2 = (bf16[512,1024]{1,0:T(8,128)(2,1)}, bf16[512,1024]{1,0:T(8,128)(2,1)S(1)}, u32[]{:S(2)}, u32[]{:S(2)}) collective-permute-start(bf16[512,1024]{1,0:T(8,128)(2,1)} %fusion.18), channel_id=1, source_target_pairs={{0,4},{4,0},{8,12},{12,8},{16,20},{20,16},{24,28},{28,24},{1,5},{5... | collective-permute-start | bytes 3145736 | tf_op jit(solution)/shard_map/ppermute | solution.py:358
  161.2 129.3 %collective-permute-start.33 = (bf16[2,128,4,512]{3,1,2,0:T(8,128)(2,1)}, bf16[2,128,4,512]{3,1,2,0:T(8,128)(2,1)}, u32[]{:S(2)}, u32[]{:S(2)}) collective-permute-start(bf16[2,128,4,512]{3,1,2,0:T(8,128)(2,1)} %pad_maximum_fusion.24), channel_id=1, source_target_pairs={{0,8},{4,12},{8,0},{12,4},{16,24},{20,28},{24,16},{28,20},{1,9},{5... | collective-permute-start | bytes 3145736 | tf_op jit(solution)/shard_map/ppermute | solution.py:358
  164.9 127.4 %collective-permute-start.31 = (bf16[2,128,4,512]{3,1,2,0:T(8,128)(2,1)}, bf16[2,128,4,512]{3,1,2,0:T(8,128)(2,1)}, u32[]{:S(2)}, u32[]{:S(2)}) collective-permute-start(bf16[2,128,4,512]{3,1,2,0:T(8,128)(2,1)} %pad_maximum_fusion.23), channel_id=1, source_target_pairs={{0,16},{4,20},{8,24},{12,28},{16,0},{20,4},{24,8},{28,12},{1,17},{... | collective-permute-start | bytes 3145736 | tf_op jit(solution)/shard_map/ppermute | solution.py:358
  168.1 134.9 %collective-permute-start.26 = (bf16[2,128,4,512]{3,1,2,0:T(8,128)(2,1)}, bf16[2,128,4,512]{3,1,2,0:T(8,128)(2,1)}, u32[]{:S(2)}, u32[]{:S(2)}) collective-permute-start(bf16[2,128,4,512]{3,1,2,0:T(8,128)(2,1)} %pad_maximum_fusion.21), channel_id=1, source_target_pairs={{0,8},{4,12},{8,0},{12,4},{16,24},{20,28},{24,16},{28,20},{1,9},{5... | collective-permute-start | bytes 3145736 | tf_op jit(solution)/shard_map/ppermute | solution.py:358
  177.9 126.7 %collective-permute-start.24 = (bf16[2,128,4,512]{3,1,2,0:T(8,128)(2,1)}, bf16[2,128,4,512]{3,1,2,0:T(8,128)(2,1)}, u32[]{:S(2)}, u32[]{:S(2)}) collective-permute-start(bf16[2,128,4,512]{3,1,2,0:T(8,128)(2,1)} %pad_maximum_fusion.20), channel_id=1, source_target_pairs={{0,16},{4,20},{8,24},{12,28},{16,0},{20,4},{24,8},{28,12},{1,17},{... | collective-permute-start | bytes 3145736 | tf_op jit(solution)/shard_map/ppermute | solution.py:358
  378.8 49.5 %collective-permute-start.34 = (bf16[512,1024]{1,0:T(8,128)(2,1)}, bf16[512,1024]{1,0:T(8,128)(2,1)}, u32[]{:S(2)}, u32[]{:S(2)}) collective-permute-start(bf16[512,1024]{1,0:T(8,128)(2,1)} %select_convert_fusion.2), channel_id=1, source_target_pairs={{0,4},{4,0},{8,12},{12,8},{16,20},{20,16},{24,28},{28,24},{1,5},{5... | collective-permute-start | bytes 3145736 | tf_op jit(solution)/shard_map/ppermute | solution.py:358
  379.3 45.2 %collective-permute-start.40 = (bf16[512,1024]{1,0:T(8,128)(2,1)}, bf16[512,1024]{1,0:T(8,128)(2,1)}, u32[]{:S(2)}, u32[]{:S(2)}) collective-permute-start(bf16[512,1024]{1,0:T(8,128)(2,1)} %select_convert_fusion.1), channel_id=1, source_target_pairs={{0,4},{4,0},{8,12},{12,8},{16,20},{20,16},{24,28},{28,24},{1,5},{5... | collective-permute-start | bytes 3145736 | tf_op jit(solution)/shard_map/ppermute | solution.py:358
  417.0 47.2 %collective-permute-start.79 = (bf16[2,128,2048]{1,2,0:T(8,128)(2,1)}, bf16[2,128,2048]{1,2,0:T(8,128)(2,1)S(1)}, u32[]{:S(2)}, u32[]{:S(2)}) collective-permute-start(bf16[2,128,2048]{1,2,0:T(8,128)(2,1)} %select_bitcast_fusion.2), channel_id=1, source_target_pairs={{0,8},{4,12},{8,0},{12,4},{16,24},{20,28},{24,16},{28,20},{1,9},{5... | collective-permute-start | bytes 3145736 | tf_op jit(solution)/shard_map/ppermute | solution.py:358
  423.1 46.2 %collective-permute-start.93 = (bf16[2,128,2048]{1,2,0:T(8,128)(2,1)S(1)}, bf16[2,128,2048]{1,2,0:T(8,128)(2,1)S(1)}, u32[]{:S(2)}, u32[]{:S(2)}) collective-permute-start(bf16[2,128,2048]{1,2,0:T(8,128)(2,1)S(1)} %select_bitcast_fusion), channel_id=1, source_target_pairs={{0,8},{4,12},{8,0},{12,4},{16,24},{20,28},{24,16},{28,20},{1,9},{5... | collective-permute-start | bytes 3145736 | tf_op jit(solution)/shard_map/ppermute | solution.py:358
  424.5 38.7 %collective-permute-start.91 = (bf16[2,128,2048]{1,2,0:T(8,128)(2,1)S(1)}, bf16[2,128,2048]{1,2,0:T(8,128)(2,1)S(1)}, u32[]{:S(2)}, u32[]{:S(2)}) collective-permute-start(bf16[2,128,2048]{1,2,0:T(8,128)(2,1)S(1)} %copy-done.65), channel_id=1, source_target_pairs={{0,16},{4,20},{8,24},{12,28},{16,0},{20,4},{24,8},{28,12},{1,17},{... | collective-permute-start | bytes 3145736 | tf_op jit(solution)/shard_map/ppermute | solution.py:358
  431.9 82.4 %collective-permute-start.35 = (bf16[256,1024]{1,0:T(8,128)(2,1)}, bf16[256,1024]{1,0:T(8,128)(2,1)}, u32[]{:S(2)}, u32[]{:S(2)}) collective-permute-start(bf16[256,1024]{1,0:T(8,128)(2,1)} %get-tuple-element.155), channel_id=1, source_target_pairs={{1,0},{0,1},{5,2},{4,3},{3,4},{2,5},{7,6},{6,7},{9,8},{8,9},{13,10... | collective-permute-start | bytes 1572872 | tf_op jit(solution)/shard_map/ppermute | solution.py:400
  440.9 73.7 %collective-permute-start.36 = (bf16[256,1024]{1,0:T(8,128)(2,1)}, bf16[256,1024]{1,0:T(8,128)(2,1)}, u32[]{:S(2)}, u32[]{:S(2)}) collective-permute-start(bf16[256,1024]{1,0:T(8,128)(2,1)} %get-tuple-element.156), channel_id=1, source_target_pairs={{0,0},{1,1},{4,2},{5,3},{2,4},{3,5},{6,6},{7,7},{8,8},{9,9},{12,10... | collective-permute-start | bytes 1572872 | tf_op jit(solution)/shard_map/ppermute | solution.py:400
  464.3 94.9 %collective-permute-start.41 = (bf16[512,1024]{1,0:T(8,128)(2,1)}, bf16[512,1024]{1,0:T(8,128)(2,1)}, u32[]{:S(2)}, u32[]{:S(2)}) collective-permute-start(bf16[512,1024]{1,0:T(8,128)(2,1)} %get-tuple-element.97), channel_id=1, source_target_pairs={{0,4},{4,0},{8,12},{12,8},{16,20},{20,16},{24,28},{28,24},{1,5},{5... | collective-permute-start | bytes 3145736 | tf_op jit(solution)/shard_map/ppermute | solution.py:358
  519.3 36.7 %collective-permute-start.96 = (bf16[2,128,512]{2,1,0:T(8,128)(2,1)S(1)}, bf16[2,128,512]{2,1,0:T(8,128)(2,1)S(1)}, u32[]{:S(2)}, u32[]{:S(2)}) collective-permute-start(bf16[2,128,512]{2,1,0:T(8,128)(2,1)S(1)} %get-tuple-element.139), channel_id=1, source_target_pairs={{0,2},{1,3},{2,0},{3,1},{4,6},{5,7},{6,4},{7,5},{8,10},{9,11},{10,... | collective-permute-start | bytes 786440 | tf_op jit(solution)/shard_map/ppermute | solution.py:362
  727.7 45.3 %collective-permute-start.42 = (bf16[512,1024]{1,0:T(8,128)(2,1)}, bf16[512,1024]{1,0:T(8,128)(2,1)}, u32[]{:S(2)}, u32[]{:S(2)}) collective-permute-start(bf16[512,1024]{1,0:T(8,128)(2,1)} %select_convert_fusion), channel_id=1, source_target_pairs={{0,4},{4,0},{8,12},{12,8},{16,20},{20,16},{24,28},{28,24},{1,5},{5... | collective-permute-start | bytes 3145736 | tf_op jit(solution)/shard_map/ppermute | solution.py:358
  730.6 40.9 %collective-permute-start.52 = (bf16[2,128,1536]{1,2,0:T(8,128)(2,1)}, bf16[2,128,1536]{1,2,0:T(8,128)(2,1)}, u32[]{:S(2)}, u32[]{:S(2)}) collective-permute-start(bf16[2,128,1536]{1,2,0:T(8,128)(2,1)} %select_bitcast_fusion.12), channel_id=1, source_target_pairs={{0,8},{4,12},{8,0},{12,4},{16,24},{20,28},{24,16},{28,20},{1,9},{5... | collective-permute-start | bytes 2359304 | tf_op jit(solution)/shard_map/ppermute | solution.py:358
  (167 other events, 1919.7 us)

commit v2 on v1

--- a/solution.py
+++ b/solution.py
@@ -3,6 +3,8 @@
 import jax
 import jax.numpy as jnp
 from jax import lax
+from jax.experimental import pallas as pl
+from jax.experimental.pallas import tpu as pltpu
 from jax.sharding import PartitionSpec as P
 
 HD = 64
@@ -347,6 +349,133 @@
     )
 
 
+def lane_swap(values):
+    even = lax.broadcasted_iota(jnp.int32, values.shape, 1) % 2 == 0
+    return jnp.where(even, pltpu.roll(values, 127, 1), pltpu.roll(values, 1, 1))
+
+
+def attend_kernel(first_ref, weight_ref, bias_ref, cos_ref, sin_ref, qkv_ref, heads_ref, turned_ref, log_ref):
+    low = jnp.bfloat16
+    packed = jnp.dot(first_ref[...], weight_ref[...], preferred_element_type=jnp.float32) + bias_ref[...]
+    cosine, sine = cos_ref[...], sin_ref[...]
+
+    def rotate(values):
+        return values * cosine + lane_swap(values) * sine
+
+    query = (rotate(packed[:, :128]).astype(low).astype(jnp.float32) * 0.125).astype(low)
+    key = rotate(packed[:, 128:256]).astype(low)
+    value = packed[:, 256:]
+    qkv_ref[:, :128] = query
+    qkv_ref[:, 128:256] = key
+    qkv_ref[:, 256:] = value.astype(low)
+    value = jnp.transpose(value).astype(low)
+    first_head = lax.broadcasted_iota(jnp.int32, key.shape, 1) < HD
+    for head in range(2):
+        mine = slice(head * HD, (head + 1) * HD)
+        key_here = jnp.where(first_head == (head == 0), key, jnp.zeros_like(key))
+        scores = contract(key_here, query, 1, 1)
+        top = jnp.max(scores, axis=0, keepdims=True)
+        expo = jnp.exp(scores - top)
+        total = jnp.sum(expo, axis=0, keepdims=True)
+        summed = jnp.dot(value[mine], expo.astype(low), preferred_element_type=jnp.float32)
+        turned_ref[0, mine] = summed / total
+        log_ref[0, head : head + 1] = top + jnp.log(total)
+    heads_ref[...] = jnp.transpose(turned_ref[0]).astype(low)
+
+
+def attend(first, weight, bias, cosine, sine):
+    length, width = first.shape
+    pairs = weight.shape[1] // 384
+    return pl.pallas_call(
+        attend_kernel,
+        grid=(pairs,),
+        in_specs=[
+            pl.BlockSpec((length, width), lambda i: (0, 0)),
+            pl.BlockSpec((width, 384), lambda i: (0, i)),
+            pl.BlockSpec((1, 384), lambda i: (0, i)),
+            pl.BlockSpec((length, 128), lambda i: (0, 0)),
+            pl.BlockSpec((length, 128), lambda i: (0, 0)),
+        ],
+        out_specs=[
+            pl.BlockSpec((length, 384), lambda i: (0, i)),
+            pl.BlockSpec((length, 128), lambda i: (0, i)),
+            pl.BlockSpec((1, 128, length), lambda i: (i, 0, 0)),
+            pl.BlockSpec((1, 2, length), lambda i: (i, 0, 0)),
+        ],
+        out_shape=[
+            jax.ShapeDtypeStruct((length, 384 * pairs), jnp.bfloat16),
+            jax.ShapeDtypeStruct((length, 128 * pairs), jnp.bfloat16),
+            jax.ShapeDtypeStruct((pairs, 128, length), jnp.float32),
+            jax.ShapeDtypeStruct((pairs, 2, length), jnp.float32),
+        ],
+        name="attend",
+    )(first, weight, bias.reshape(1, -1), cosine, sine)
+
+
+def attend_back_kernel(qkv_ref, grad_ref, turned_ref, log_ref, cos_ref, sin_ref, out_ref, bias_ref):
+    low = jnp.bfloat16
+    query = qkv_ref[:, :128]
+    key = qkv_ref[:, 128:256]
+    value = qkv_ref[:, 256:]
+    grad = grad_ref[...]
+    key_turned = jnp.transpose(key.astype(jnp.float32)).astype(low)
+    product = jnp.transpose(grad.astype(jnp.float32)) * turned_ref[0]
+    first_head = lax.broadcasted_iota(jnp.int32, key.shape, 1) < HD
+    zero = jnp.zeros_like(key)
+    query_grads, key_grads, value_grads = [], [], []
+    for head in range(2):
+        mine = slice(head * HD, (head + 1) * HD)
+        here = first_head == (head == 0)
+        delta = jnp.sum(product[mine], axis=0, keepdims=True)
+        scores = contract(jnp.where(here, key, zero), query, 1, 1)
+        probs = jnp.exp(scores - log_ref[0, head : head + 1])
+        grad_probs = contract(jnp.where(here, value, zero), grad, 1, 1)
+        grad_scores = (probs * (grad_probs - delta)).astype(low)
+        value_grads.append(jnp.dot(probs.astype(low), grad, preferred_element_type=jnp.float32))
+        key_grads.append(jnp.dot(grad_scores, query, preferred_element_type=jnp.float32))
+        query_grads.append(jnp.dot(key_turned[mine], grad_scores, preferred_element_type=jnp.float32))
+    cosine, sine = cos_ref[...], sin_ref[...]
+
+    def rotate_back(values):
+        return values * cosine + lane_swap(values * sine)
+
+    parts = [
+        rotate_back(jnp.transpose(jnp.concatenate(query_grads, axis=0)) * 0.125),
+        rotate_back(jnp.where(first_head, key_grads[0], key_grads[1])),
+        jnp.where(first_head, value_grads[0], value_grads[1]),
+    ]
+    for at, part in enumerate(parts):
+        part = part.astype(low)
+        out_ref[:, at * 128 : (at + 1) * 128] = part
+        bias_ref[:, at * 128 : (at + 1) * 128] = jnp.sum(part.astype(jnp.float32), axis=0, keepdims=True)
+
+
+def attend_back(qkv, grad, turned, logs, cosine, sine):
+    length = qkv.shape[0]
+    pairs = qkv.shape[1] // 384
+    return pl.pallas_call(
+        attend_back_kernel,
+        grid=(pairs,),
+        in_specs=[
+            pl.BlockSpec((length, 384), lambda i: (0, i)),
+            pl.BlockSpec((length, 128), lambda i: (0, i)),
+            pl.BlockSpec((1, 128, length), lambda i: (i, 0, 0)),
+            pl.BlockSpec((1, 2, length), lambda i: (i, 0, 0)),
+            pl.BlockSpec((length, 128), lambda i: (0, 0)),
+            pl.BlockSpec((length, 128), lambda i: (0, 0)),
+        ],
+        out_specs=[
+            pl.BlockSpec((length, 384), lambda i: (0, i)),
+            pl.BlockSpec((1, 384), lambda i: (0, i)),
+        ],
+        out_shape=[
+            jax.ShapeDtypeStruct((length, 384 * pairs), jnp.bfloat16),
+            jax.ShapeDtypeStruct((1, 384 * pairs), jnp.float32),
+        ],
+        name="attend_back",
+    )(qkv, grad, turned, logs, cosine, sine)
+
+
 SWAP_CORE, SWAP_X, SWAP_Y = 1, 2, 4
 
 
@@ -435,11 +564,9 @@
     own_rows = qkv_weight.shape[0]
     heads_here = qkv_weight.shape[1] // (3 * HD)
     half_heads = heads_here // 2
-    heads = 4 * half_heads
     qkv_cols = half_heads * 3 * HD
     out_cols = out_weight.shape[1] // 2
     unit_cols = fc1_weight.shape[1] // 2
-    factor = 1.0 / math.sqrt(HD)
     low = jnp.bfloat16
 
     def first_half(values):
@@ -518,30 +645,10 @@
         sent = pick(core == 1, halves[1], halves[0]).astype(low)
         return pick(core == 1, halves[0], halves[1]) + swap(sent, SWAP_CORE).astype(jnp.float32)
 
-    cosine, sine = rotary_tables(length)
-    cosine = cosine[:, None, :]
-    sine = sine[:, None, :]
-
-    def rotate(values):
-        return values * cosine + pair_swap(values) * sine
-
-    def rotate_back(values):
-        return values * cosine + pair_swap(values * sine)
+    cosine, sine = (jnp.concatenate([item, item], axis=1) for item in rotary_tables(length))
 
     first_all = both_halves(norm_rows(tokens, attn_gain, attn_shift).astype(low))
-    packed = jnp.dot(first_all, weight_qkv, preferred_element_type=jnp.float32) + bias_qkv
-    packed = packed.reshape(length, 4, 3, half_heads, HD)
-    query = rotate(packed[:, :, 0].reshape(length, heads, HD)).astype(low)
-    key = rotate(packed[:, :, 1].reshape(length, heads, HD)).astype(low)
-    value = packed[:, :, 2].reshape(length, heads, HD).astype(low)
-    scores = jnp.einsum("qhd,khd->hqk", query, key, preferred_element_type=jnp.float32) * factor
-    row_max = jnp.max(scores, axis=-1, keepdims=True)
-    expo = jnp.exp(scores - row_max)
-    row_total = jnp.sum(expo, axis=-1, keepdims=True)
-    weights_low = (expo / row_total).astype(low)
-    heads_out = jnp.einsum("hqk,khd->qhd", weights_low, value, preferred_element_type=jnp.float32)
-    heads_out = heads_out.reshape(length, heads * HD).astype(low)
-    log_total = row_max + jnp.log(row_total)
+    qkv, heads_out, turned, log_total = attend(first_all, weight_qkv, bias_qkv, cosine, sine)
     resid = tokens + part_sum(contract(heads_out, weight_out, 1, 1)) + out_bias
     second_all = both_halves(norm_rows(resid, mlp_gain, mlp_shift).astype(low))
     hidden = jnp.dot(second_all, weight_up, preferred_element_type=jnp.float32) + bias_up
@@ -584,24 +691,8 @@
     resid_all = both_halves(grad_resid.astype(low))
     grad_out_weight = to_owner(contract(resid_all, heads_out, 0, 0), out_cols)
     grad_heads = jnp.dot(resid_all, weight_out, preferred_element_type=jnp.float32).astype(low)
-    grad_heads = grad_heads.reshape(length, heads, HD)
-    scores = jnp.einsum("qhd,khd->hqk", query, key, preferred_element_type=jnp.float32) * factor
-    probs = jnp.exp(scores - log_total)
-    grad_value = jnp.einsum(
-        "hqk,qhd->khd", probs.astype(low), grad_heads, preferred_element_type=jnp.float32
-    )
-    grad_probs = jnp.einsum("qhd,khd->hqk", grad_heads, value, preferred_element_type=jnp.float32)
-    grad_scores = (
-        probs * (grad_probs - jnp.sum(probs * grad_probs, axis=-1, keepdims=True))
-    ).astype(low)
-    grad_query = factor * jnp.einsum("hqk,khd->qhd", grad_scores, key, preferred_element_type=jnp.float32)
-    grad_key = factor * jnp.einsum("hqk,qhd->khd", grad_scores, query, preferred_element_type=jnp.float32)
-    kinds = [
-        item.reshape(length, 4, 1, half_heads, HD)
-        for item in (rotate_back(grad_query), rotate_back(grad_key), grad_value)
-    ]
-    grad_packed = jnp.concatenate(kinds, axis=2).reshape(length, 4 * qkv_cols).astype(low)
-    sum_qkv_bias = jnp.sum(grad_packed, axis=0, dtype=jnp.float32)
+    grad_packed, sum_qkv_bias = attend_back(qkv, grad_heads, turned, log_total, cosine, sine)
+    sum_qkv_bias = sum_qkv_bias.reshape(-1)
     grad_qkv_weight = by_head(to_owner(contract(first_all, grad_packed, 0, 0), qkv_cols))
     grad_first = part_sum(contract(grad_packed, weight_qkv, 1, 1))
     first_pull = jax.vjp(norm_rows, tokens, attn_gain, attn_shift)[1]

time: 849 us -> 697 us (0.82)
  matrix products: 169 us -> 81 us
  local copies, waits for them, and re-layouts: 154 us -> 91 us
  other arithmetic: 150 us -> 88.8 us
  Pallas kernels: 0 us -> 46.6 us
  waiting for transfers between devices: 227 us -> 238 us
    dot_general x7 -> x0, matrix products: 93.7 us -> none  [the longest x1 22.4 us: clip_body(): jnp.einsum('qhd,khd->hqk', grad_heads, value, preferred_element_type=jnp....]
    pallas_call x0 -> x2, Pallas kernels: none -> 46.6 us  [the longest x1 25.9 us: attend_back(): pl.pallas_call(attend_back_kernel, grid=(pairs,), in_specs=[pl.BlockSpec(...]
    rev x4 -> x0, local copies, waits for them, and re-layouts: 44.2 us -> none  [pair_swap(): return paired[..., ::-1].reshape(shape)]
    convert_element_type x2 -> x0, other arithmetic: 32.2 us -> none  [the longest x1 28.2 us: clip_body(): grad_scores = (probs * (grad_probs - jnp.sum(probs * grad_probs, axis=-1,...]
    reshape x6 -> x7, local copies, waits for them, and re-layouts: 22.1 us -> 0.87 us  [the longest x6 0.82 us: rotary_tables(): jnp.repeat(coordinate[:, None] * omega[None, :], 2, axis=1)]
    reduce_sum x2 -> x0, other arithmetic: 14.2 us -> none  [the longest x1 13.6 us: clip_body(): row_total = jnp.sum(expo, axis=-1, keepdims=True)]
    unnamed x202 -> x201, local copies, waits for them, and re-layouts: 30.7 us -> 43.6 us
    another operation x8 -> x0, local copies, waits for them, and re-layouts: 12.5 us -> none  [the longest x6 6.81 us: to_owner(): both = jnp.stack([even, odd]).reshape(2, own_rows, 4, cols)]
  transfers between devices with their start and end apart: 99 -> 99, of which waited for: 38 -> 39; matrix products, arithmetic and copies ran while one was open for 30% -> 24% of each run, Pallas kernels for 0% -> 3%
where the time goes in v2:
time: 697 us; the launch traced here: 687 us
  waiting for transfers between devices  238 us (34%)
  starting transfers between devices  139 us (20%)
  local copies, waits for them, and re-layouts  91 us (13%)
  other arithmetic  88.8 us (13%)
  matrix products  81 us (12%)
  Pallas kernels  46.6 us (7%)
    ppermute x57, waiting for transfers between devices, swap(): return lax.ppermute(values, 'dp', [(i, i ^ bit) for i in range(8)])  101 us
    ppermute x30, waiting for transfers between devices, shift(): lax.ppermute(values, 'tensor', [(i, (i + step) % 4) for i in range(4)])  92 us
    ppermute x57, starting transfers between devices, swap(): return lax.ppermute(values, 'dp', [(i, i ^ bit) for i in range(8)])  69.8 us
    unnamed x201, local copies, waits for them, and re-layouts  43.6 us
    dot_general x8, matrix products, contract(): lax.dot_general(left, right, (((left_dim,), (right_dim,)), ((), ())), pre...  39.6 us
    ppermute x30, starting transfers between devices, shift(): lax.ppermute(values, 'tensor', [(i, (i + step) % 4) for i in range(4)])  30.7 us
    pallas_call x1, Pallas kernels, attend_back(): pl.pallas_call(attend_back_kernel, grid=(pairs,), in_specs=[pl.BlockSpec(...  25.9 us
    dot_general x1, matrix products, clip_body(): jnp.dot(second_all, weight_up, preferred_element_type=jnp.float32) + bias_up  25.5 us
  transfers between devices with their start and end apart: 99, of which 39 were waited for; matrix products, arithmetic and copies ran while one was open for 24% of the time, Pallas kernels for 3%

profile of v2, /device:TPU:1, one launch (start us, length us, event | category | flops | bytes accessed | tf_op | source)
XLA Modules:
  0.0 687.3 jit_solution(6477365497108764766)
XLA Ops:
  26.1 7.3 %collective-permute-done.12 = bf16[2,128,128]{1,2,0:T(8,128)(2,1)S(1)} collective-permute-done((bf16[2,128,128]{1,2,0:T(8,128)(2,1)S(1)}, bf16[2,128,128]{1,2,0:T(8,128)(2,1)S(1)}, u32[]{:S(2)}, u32[]{:S(2)}) %collective-permute-start.12) | collective-permute-done | bytes 65568 | tf_op jit(solution)/shard_map/ppermute | solution.py:491
  34.2 13.0 %collective-permute-start.38 = (bf16[256,1024]{1,0:T(8,128)(2,1)S(1)}, bf16[256,1024]{1,0:T(8,128)(2,1)S(1)}, u32[]{:S(2)}, u32[]{:S(2)}) collective-permute-start(bf16[256,1024]{1,0:T(8,128)(2,1)S(1)} %get-tuple-element.158), channel_id=1, source_target_pairs={{0,0},{1,1},{2,4},{3,5},{4,2},{5,3},{6,6},{7,7},{8,8},{9,9},{10,12... | collective-permute-start | bytes 1572872 | tf_op jit(solution)/shard_map/ppermute | solution.py:517
  55.5 21.6 %collective-permute-done.38 = bf16[256,1024]{1,0:T(8,128)(2,1)S(1)} collective-permute-done((bf16[256,1024]{1,0:T(8,128)(2,1)S(1)}, bf16[256,1024]{1,0:T(8,128)(2,1)S(1)}, u32[]{:S(2)}, u32[]{:S(2)}) %collective-permute-start.38) | collective-permute-done | bytes 524320 | tf_op jit(solution)/shard_map/ppermute | solution.py:517
  86.6 13.7 %collective-permute-done.28 = bf16[2,128,512]{1,2,0:T(8,128)(2,1)S(1)} collective-permute-done((bf16[2,128,512]{1,2,0:T(8,128)(2,1)S(1)}, bf16[2,128,512]{1,2,0:T(8,128)(2,1)S(1)}, u32[]{:S(2)}, u32[]{:S(2)}) %collective-permute-start.28) | collective-permute-done | bytes 262176 | tf_op jit(solution)/shard_map/ppermute | solution.py:491
  102.2 27.4 %collective-permute-done.21 = bf16[272,512]{0,1:T(8,128)(2,1)S(1)} collective-permute-done((bf16[272,512]{0,1:T(8,128)(2,1)S(1)}, bf16[272,512]{0,1:T(8,128)(2,1)S(1)}, u32[]{:S(2)}, u32[]{:S(2)}) %collective-permute-start.21) | collective-permute-done | bytes 278560 | tf_op jit(solution)/shard_map/ppermute | solution.py:491
  148.4 8.4 %collective-permute-done.30 = bf16[128,4,512]{0,2,1:T(8,128)(2,1)} collective-permute-done((bf16[128,4,512]{0,2,1:T(8,128)(2,1)}, bf16[128,4,512]{0,2,1:T(8,128)(2,1)}, u32[]{:S(2)}, u32[]{:S(2)}) %collective-permute-start.30) | collective-permute-done | bytes 524320 | tf_op jit(solution)/shard_map/ppermute | solution.py:487
  190.6 20.6 %attend.1 = (bf16[1024,1536]{1,0:T(8,128)(2,1)}, bf16[1024,512]{1,0:T(8,128)(2,1)}, f32[4,128,1024]{2,1,0:T(8,128)}, f32[4,2,1024]{2,1,0:T(2,128)}) custom-call(bf16[1024,1024]{1,0:T(8,128)(2,1)} %pad_maximum_fusion.3.first_ref, bf16[1024,1536]{1,0:T(8,128)(2,1)} %bitcast.397, f32[1,1536]{1,0:T(1,128)} %bitcast.475, f32[1024,128]{1,0:T(8,128)} %pad_maximum_fusion.28.cos_ref, ...), custom_call_target="tpu_custom_call" | custom-call | tf_op jit(solution)/shard_map/attend/pallas_call | solution.py:389
  225.4 7.8 %copy.141 = bf16[2,2,2,128,4,512]{5,4,3,2,1,0:T(4,128)(2,1)} copy(bf16[2,2,2,128,4,512]{3,5,4,0,1,2:T(8,128)(2,1)} %pad_maximum_fusion.1) | data formatting | bytes 8388608 | tf_op jit(solution)/shard_map/stack | solution.py:615
  250.2 7.8 %copy.138 = bf16[2,2,2,128,4,512]{5,4,3,2,1,0:T(4,128)(2,1)} copy(bf16[2,2,2,128,4,512]{3,5,4,1,0,2:T(8,128)(2,1)} %pad_maximum_fusion) | data formatting | bytes 8388608 | tf_op jit(solution)/shard_map/stack | solution.py:615
  263.5 25.5 %multiply_convert_fusion = (bf16[1024,2048]{1,0:T(8,128)(2,1)S(1)}, f32[1024,2048]{1,0:T(8,128)}, f32[1024,2048]{1,0:T(8,128)}) fusion(f32[2048]{0:T(1024)S(1)} %bitcast.477, bf16[1024,2048]{1,0:T(8,128)(2,1)S(1)} %bitcast.416, bf16[512,1024]{1,0:T(8,128)(2,1)S(1)} %get-tuple-element.116, bf16[512,1024]{1,0:T(8,128)(2,1)S(1)} %get-tuple-element.115), kind=kOutput, calls=%fused_computation.4 | convolution fusion | flops 4437573632 | bytes 27271168 | tf_op jit(solution)/shard_map/dot_general | solution.py:654
  299.8 13.7 %convert_reduce_fusion = (f32[2048]{0:T(1024)S(1)}, bf16[1024,2048]{1,0:T(8,128)(2,1)}) fusion(f32[1024,2048]{1,0:T(8,128)} %get-tuple-element.92, bf16[1024,2048]{1,0:T(8,128)(2,1)S(1)} %bitcast.413, bf16[512,1024]{1,0:T(8,128)(2,1)S(1)} %copy-done.57, bf16[512,1024]{1,0:T(8,128)(2,1)S(1)} %copy-done.56, f32[1024,2048]{1,0:T(8,128)} %get-tuple-element.247, ...), kind=kOutput, calls=%fused_computation.2 | convolution fusion | flops 4334811136 | bytes 27279360 | tf_op jit(solution)/shard_map/dot_general | solution.py:682
  313.5 6.8 fusion.126
  400.4 15.5 %collective-permute-done.91 = bf16[2,128,2048]{1,2,0:T(8,128)(2,1)S(1)} collective-permute-done((bf16[2,128,2048]{1,2,0:T(8,128)(2,1)S(1)}, bf16[2,128,2048]{1,2,0:T(8,128)(2,1)S(1)}, u32[]{:S(2)}, u32[]{:S(2)}) %collective-permute-start.91) | collective-permute-done | bytes 1048608 | tf_op jit(solution)/shard_map/ppermute | solution.py:487
  422.3 10.0 %collective-permute-done.73 = f32[4,1024]{1,0:T(4,128)S(1)} collective-permute-done((f32[4,1024]{1,0:T(4,128)S(1)}, f32[4,1024]{1,0:T(4,128)S(1)}, u32[]{:S(2)}, u32[]{:S(2)}) %collective-permute-start.73) | collective-permute-done | bytes 16416 | tf_op jit(solution)/shard_map/ppermute | solution.py:487
  445.1 7.9 %collective-permute-done.78 = bf16[128,2048]{0,1:T(8,128)(2,1)S(1)} collective-permute-done((bf16[128,2048]{0,1:T(8,128)(2,1)S(1)}, bf16[128,2048]{0,1:T(8,128)(2,1)S(1)}, u32[]{:S(2)}, u32[]{:S(2)}) %collective-permute-start.78) | collective-permute-done | bytes 524320 | tf_op jit(solution)/shard_map/ppermute | solution.py:487
  455.2 8.2 %collective-permute-done.92 = bf16[128,2048]{0,1:T(8,128)(2,1)S(1)} collective-permute-done((bf16[128,2048]{0,1:T(8,128)(2,1)S(1)}, bf16[128,2048]{0,1:T(8,128)(2,1)S(1)}, u32[]{:S(2)}, u32[]{:S(2)}) %collective-permute-start.92) | collective-permute-done | bytes 524320 | tf_op jit(solution)/shard_map/ppermute | solution.py:487
  470.6 16.1 %collective-permute-done.82 = bf16[2,128,512]{1,2,0:T(8,128)(2,1)S(1)} collective-permute-done((bf16[2,128,512]{1,2,0:T(8,128)(2,1)S(1)}, bf16[2,128,512]{1,2,0:T(8,128)(2,1)S(1)}, u32[]{:S(2)}, u32[]{:S(2)}) %collective-permute-start.82) | collective-permute-done | bytes 262176 | tf_op jit(solution)/shard_map/ppermute | solution.py:491
  486.9 9.9 %collective-permute-start.84 = (bf16[128,512]{0,1:T(8,128)(2,1)S(1)}, bf16[128,512]{0,1:T(8,128)(2,1)S(1)}, u32[]{:S(2)}, u32[]{:S(2)}) collective-permute-start(bf16[128,512]{0,1:T(8,128)(2,1)S(1)} %select_bitcast_fusion.53), channel_id=1, source_target_pairs={{0,4},{4,0},{8,12},{12,8},{16,20},{20,16},{24,28},{28,24},{1,5},{5... | collective-permute-start | bytes 393224 | tf_op jit(solution)/shard_map/ppermute | solution.py:487
  496.8 9.1 %collective-permute-done.96 = bf16[2,128,512]{1,2,0:T(8,128)(2,1)S(1)} collective-permute-done((bf16[2,128,512]{1,2,0:T(8,128)(2,1)S(1)}, bf16[2,128,512]{1,2,0:T(8,128)(2,1)S(1)}, u32[]{:S(2)}, u32[]{:S(2)}) %collective-permute-start.96) | collective-permute-done | bytes 262176 | tf_op jit(solution)/shard_map/ppermute | solution.py:491
  515.0 25.9 %attend_back.1 = (bf16[1024,1536]{1,0:T(8,128)(2,1)}, f32[1,1536]{1,0:T(1,128)}) custom-call(bf16[1024,1536]{1,0:T(8,128)(2,1)} %get-tuple-element.45.qkv_ref, bf16[1024,512]{1,0:T(8,128)(2,1)} %convolution_convert_fusion.4.grad_ref, f32[4,128,1024]{2,1,0:T(8,128)} %get-tuple-element.46.turned_ref, f32[4,2,1024]{2,1,0:T(2,128)} %get-tuple-element.47.log_ref, ...), custom_call_target="tpu_custom_call" | custom-call | tf_op jit(solution)/shard_map/attend_back/pallas_call | solution.py:456
  540.9 8.4 %fusion.127 = f32[1024,1024]{1,0:T(8,128)} fusion(bf16[1024,1536]{1,0:T(8,128)(2,1)} %get-tuple-element.48, bf16[1024,1536]{1,0:T(8,128)(2,1)} %bitcast.398), kind=kOutput, calls=%fused_computation.412 | convolution fusion | flops 3221225472 | bytes 10485760 | tf_op jit(solution)/shard_map/dot_general | solution.py:46
  587.8 13.9 %collective-permute-done.65 = bf16[128,512]{0,1:T(8,128)(2,1)S(1)} collective-permute-done((bf16[128,512]{0,1:T(8,128)(2,1)S(1)}, bf16[128,512]{0,1:T(8,128)(2,1)S(1)}, u32[]{:S(2)}, u32[]{:S(2)}) %collective-permute-start.65) | collective-permute-done | bytes 131104 | tf_op jit(solution)/shard_map/ppermute | solution.py:487
  654.1 7.9 %collective-permute-done.55 = bf16[2,128,384]{1,2,0:T(8,128)(2,1)S(1)} collective-permute-done((bf16[2,128,384]{1,2,0:T(8,128)(2,1)S(1)}, bf16[2,128,384]{1,2,0:T(8,128)(2,1)S(1)}, u32[]{:S(2)}, u32[]{:S(2)}) %collective-permute-start.55) | collective-permute-done | bytes 196640 | tf_op jit(solution)/shard_map/ppermute | solution.py:491
  670.6 14.8 %collective-permute-done.44 = bf16[256,1024]{1,0:T(8,128)(2,1)S(1)} collective-permute-done((bf16[256,1024]{1,0:T(8,128)(2,1)S(1)}, bf16[256,1024]{1,0:T(8,128)(2,1)S(1)}, u32[]{:S(2)}, u32[]{:S(2)}) %collective-permute-start.44) | collective-permute-done | bytes 524320 | tf_op jit(solution)/shard_map/ppermute | solution.py:529
  (615 shorter events, 362.8 us)
Async XLA Ops:
  6.1 41.4 %collective-permute-start = (bf16[256,1024]{1,0:T(8,128)(2,1)}, bf16[256,1024]{1,0:T(8,128)(2,1)}, u32[]{:S(2)}, u32[]{:S(2)}) collective-permute-start(bf16[256,1024]{1,0:T(8,128)(2,1)} %get-tuple-element.169), channel_id=1, source_target_pairs={{0,1},{1,0},{2,5},{3,4},{4,3},{5,2},{6,7},{7,6},{8,9},{9,8},{10,13... | collective-permute-start | bytes 1572872 | tf_op jit(solution)/shard_map/ppermute | solution.py:517
  10.8 36.8 %collective-permute-start.1 = (bf16[256,1024]{1,0:T(8,128)(2,1)S(1)}, bf16[256,1024]{1,0:T(8,128)(2,1)}, u32[]{:S(2)}, u32[]{:S(2)}) collective-permute-start(bf16[256,1024]{1,0:T(8,128)(2,1)S(1)} %get-tuple-element.170), channel_id=1, source_target_pairs={{0,0},{1,1},{2,4},{3,5},{4,2},{5,3},{6,6},{7,7},{8,8},{9,9},{10,12... | collective-permute-start | bytes 1572872 | tf_op jit(solution)/shard_map/ppermute | solution.py:517
  34.2 42.9 %collective-permute-start.38 = (bf16[256,1024]{1,0:T(8,128)(2,1)S(1)}, bf16[256,1024]{1,0:T(8,128)(2,1)S(1)}, u32[]{:S(2)}, u32[]{:S(2)}) collective-permute-start(bf16[256,1024]{1,0:T(8,128)(2,1)S(1)} %get-tuple-element.158), channel_id=1, source_target_pairs={{0,0},{1,1},{2,4},{3,5},{4,2},{5,3},{6,6},{7,7},{8,8},{9,9},{10,12... | collective-permute-start | bytes 1572872 | tf_op jit(solution)/shard_map/ppermute | solution.py:517
  47.5 36.8 %collective-permute-start.4 = (bf16[272,384]{1,0:T(8,128)(2,1)S(1)}, bf16[272,384]{1,0:T(8,128)(2,1)S(1)}, u32[]{:S(2)}, u32[]{:S(2)}) collective-permute-start(bf16[272,384]{1,0:T(8,128)(2,1)S(1)} %get-tuple-element.214), channel_id=1, source_target_pairs={{0,1},{1,2},{2,3},{3,0},{4,5},{5,6},{6,7},{7,4},{8,9},{9,10},{10,1... | collective-permute-start | bytes 626696 | tf_op jit(solution)/shard_map/ppermute | solution.py:491
  47.6 36.7 %collective-permute-start.6 = (bf16[272,384]{1,0:T(8,128)(2,1)S(1)}, bf16[272,384]{1,0:T(8,128)(2,1)S(1)}, u32[]{:S(2)}, u32[]{:S(2)}) collective-permute-start(bf16[272,384]{1,0:T(8,128)(2,1)S(1)} %get-tuple-element.214), channel_id=1, source_target_pairs={{0,3},{1,0},{2,1},{3,2},{4,7},{5,4},{6,5},{7,6},{8,11},{9,8},{10,9... | collective-permute-start | bytes 626696 | tf_op jit(solution)/shard_map/ppermute | solution.py:491
  84.3 45.3 %collective-permute-start.21 = (bf16[272,512]{0,1:T(8,128)(2,1)S(1)}, bf16[272,512]{0,1:T(8,128)(2,1)S(1)}, u32[]{:S(2)}, u32[]{:S(2)}) collective-permute-start(bf16[272,512]{0,1:T(8,128)(2,1)S(1)} %get-tuple-element.191), channel_id=1, source_target_pairs={{0,2},{1,3},{2,0},{3,1},{4,6},{5,7},{6,4},{7,5},{8,10},{9,11},{10,... | collective-permute-start | bytes 835592 | tf_op jit(solution)/shard_map/ppermute | solution.py:491
  84.3 46.5 %collective-permute-start.20 = (bf16[272,512]{0,1:T(8,128)(2,1)S(1)}, bf16[272,512]{0,1:T(8,128)(2,1)S(1)}, u32[]{:S(2)}, u32[]{:S(2)}) collective-permute-start(bf16[272,512]{0,1:T(8,128)(2,1)S(1)} %get-tuple-element.191), channel_id=1, source_target_pairs={{0,1},{1,2},{2,3},{3,0},{4,5},{5,6},{6,7},{7,4},{8,9},{9,10},{10,1... | collective-permute-start | bytes 835592 | tf_op jit(solution)/shard_map/ppermute | solution.py:491
  100.2 76.7 %collective-permute-start.39 = (bf16[512,1024]{1,0:T(8,128)(2,1)}, bf16[512,1024]{1,0:T(8,128)(2,1)}, u32[]{:S(2)}, u32[]{:S(2)}) collective-permute-start(bf16[512,1024]{1,0:T(8,128)(2,1)} %pad_maximum_fusion.24), channel_id=1, source_target_pairs={{0,4},{4,0},{8,12},{12,8},{16,20},{20,16},{24,28},{28,24},{1,5},{5... | collective-permute-start | bytes 3145736 | tf_op jit(solution)/shard_map/ppermute | solution.py:487
  100.6 71.1 %collective-permute-start.2 = (bf16[512,1024]{1,0:T(8,128)(2,1)}, bf16[512,1024]{1,0:T(8,128)(2,1)}, u32[]{:S(2)}, u32[]{:S(2)}) collective-permute-start(bf16[512,1024]{1,0:T(8,128)(2,1)} %fusion.13), channel_id=1, source_target_pairs={{0,4},{4,0},{8,12},{12,8},{16,20},{20,16},{24,28},{28,24},{1,5},{5... | collective-permute-start | bytes 3145736 | tf_op jit(solution)/shard_map/ppermute | solution.py:487
  168.1 52.0 %collective-permute-start.33 = (bf16[2,128,4,512]{1,3,2,0:T(8,128)(2,1)}, bf16[2,128,4,512]{1,3,2,0:T(8,128)(2,1)S(1)}, u32[]{:S(2)}, u32[]{:S(2)}) collective-permute-start(bf16[2,128,4,512]{1,3,2,0:T(8,128)(2,1)} %pad_maximum_fusion.22), channel_id=1, source_target_pairs={{0,8},{4,12},{8,0},{12,4},{16,24},{20,28},{24,16},{28,20},{1,9},{5... | collective-permute-start | bytes 3145736 | tf_op jit(solution)/shard_map/ppermute | solution.py:487
  171.8 48.7 %collective-permute-start.31 = (bf16[2,128,4,512]{1,3,2,0:T(8,128)(2,1)}, bf16[2,128,4,512]{1,3,2,0:T(8,128)(2,1)}, u32[]{:S(2)}, u32[]{:S(2)}) collective-permute-start(bf16[2,128,4,512]{1,3,2,0:T(8,128)(2,1)} %pad_maximum_fusion.21), channel_id=1, source_target_pairs={{0,16},{4,20},{8,24},{12,28},{16,0},{20,4},{24,8},{28,12},{1,17},{... | collective-permute-start | bytes 3145736 | tf_op jit(solution)/shard_map/ppermute | solution.py:487
  176.9 66.8 %collective-permute-start.26 = (bf16[2,128,4,512]{1,3,2,0:T(8,128)(2,1)}, bf16[2,128,4,512]{1,3,2,0:T(8,128)(2,1)}, u32[]{:S(2)}, u32[]{:S(2)}) collective-permute-start(bf16[2,128,4,512]{1,3,2,0:T(8,128)(2,1)} %pad_maximum_fusion.19), channel_id=1, source_target_pairs={{0,8},{4,12},{8,0},{12,4},{16,24},{20,28},{24,16},{28,20},{1,9},{5... | collective-permute-start | bytes 3145736 | tf_op jit(solution)/shard_map/ppermute | solution.py:487
  184.8 60.5 %collective-permute-start.24 = (bf16[2,128,4,512]{1,3,2,0:T(8,128)(2,1)}, bf16[2,128,4,512]{1,3,2,0:T(8,128)(2,1)}, u32[]{:S(2)}, u32[]{:S(2)}) collective-permute-start(bf16[2,128,4,512]{1,3,2,0:T(8,128)(2,1)} %pad_maximum_fusion.18), channel_id=1, source_target_pairs={{0,16},{4,20},{8,24},{12,28},{16,0},{20,4},{24,8},{28,12},{1,17},{... | collective-permute-start | bytes 3145736 | tf_op jit(solution)/shard_map/ppermute | solution.py:487
  328.8 52.2 %collective-permute-start.34 = (bf16[512,1024]{1,0:T(8,128)(2,1)}, bf16[512,1024]{1,0:T(8,128)(2,1)}, u32[]{:S(2)}, u32[]{:S(2)}) collective-permute-start(bf16[512,1024]{1,0:T(8,128)(2,1)} %select_convert_fusion.2), channel_id=1, source_target_pairs={{0,4},{4,0},{8,12},{12,8},{16,20},{20,16},{24,28},{28,24},{1,5},{5... | collective-permute-start | bytes 3145736 | tf_op jit(solution)/shard_map/ppermute | solution.py:487
  329.5 47.8 %collective-permute-start.40 = (bf16[512,1024]{1,0:T(8,128)(2,1)}, bf16[512,1024]{1,0:T(8,128)(2,1)}, u32[]{:S(2)}, u32[]{:S(2)}) collective-permute-start(bf16[512,1024]{1,0:T(8,128)(2,1)} %select_convert_fusion.1), channel_id=1, source_target_pairs={{0,4},{4,0},{8,12},{12,8},{16,20},{20,16},{24,28},{28,24},{1,5},{5... | collective-permute-start | bytes 3145736 | tf_op jit(solution)/shard_map/ppermute | solution.py:487
  369.7 47.4 %collective-permute-start.79 = (bf16[2,128,2048]{1,2,0:T(8,128)(2,1)}, bf16[2,128,2048]{1,2,0:T(8,128)(2,1)S(1)}, u32[]{:S(2)}, u32[]{:S(2)}) collective-permute-start(bf16[2,128,2048]{1,2,0:T(8,128)(2,1)} %select_bitcast_fusion.2), channel_id=1, source_target_pairs={{0,8},{4,12},{8,0},{12,4},{16,24},{20,28},{24,16},{28,20},{1,9},{5... | collective-permute-start | bytes 3145736 | tf_op jit(solution)/shard_map/ppermute | solution.py:487
  375.8 46.2 %collective-permute-start.93 = (bf16[2,128,2048]{1,2,0:T(8,128)(2,1)S(1)}, bf16[2,128,2048]{1,2,0:T(8,128)(2,1)S(1)}, u32[]{:S(2)}, u32[]{:S(2)}) collective-permute-start(bf16[2,128,2048]{1,2,0:T(8,128)(2,1)S(1)} %select_bitcast_fusion), channel_id=1, source_target_pairs={{0,8},{4,12},{8,0},{12,4},{16,24},{20,28},{24,16},{28,20},{1,9},{5... | collective-permute-start | bytes 3145736 | tf_op jit(solution)/shard_map/ppermute | solution.py:487
  377.3 38.7 %collective-permute-start.91 = (bf16[2,128,2048]{1,2,0:T(8,128)(2,1)S(1)}, bf16[2,128,2048]{1,2,0:T(8,128)(2,1)S(1)}, u32[]{:S(2)}, u32[]{:S(2)}) collective-permute-start(bf16[2,128,2048]{1,2,0:T(8,128)(2,1)S(1)} %copy-done.62), channel_id=1, source_target_pairs={{0,16},{4,20},{8,24},{12,28},{16,0},{20,4},{24,8},{28,12},{1,17},{... | collective-permute-start | bytes 3145736 | tf_op jit(solution)/shard_map/ppermute | solution.py:487
  383.7 79.9 %collective-permute-start.35 = (bf16[256,1024]{1,0:T(8,128)(2,1)S(1)}, bf16[256,1024]{1,0:T(8,128)(2,1)S(1)}, u32[]{:S(2)}, u32[]{:S(2)}) collective-permute-start(bf16[256,1024]{1,0:T(8,128)(2,1)S(1)} %get-tuple-element.161), channel_id=1, source_target_pairs={{1,0},{0,1},{5,2},{4,3},{3,4},{2,5},{7,6},{6,7},{9,8},{8,9},{13,10... | collective-permute-start | bytes 1572872 | tf_op jit(solution)/shard_map/ppermute | solution.py:529
  393.5 71.6 %collective-permute-start.36 = (bf16[256,1024]{1,0:T(8,128)(2,1)S(1)}, bf16[256,1024]{1,0:T(8,128)(2,1)S(1)}, u32[]{:S(2)}, u32[]{:S(2)}) collective-permute-start(bf16[256,1024]{1,0:T(8,128)(2,1)S(1)} %get-tuple-element.162), channel_id=1, source_target_pairs={{0,0},{1,1},{4,2},{5,3},{2,4},{3,5},{6,6},{7,7},{8,8},{9,9},{12,10... | collective-permute-start | bytes 1572872 | tf_op jit(solution)/shard_map/ppermute | solution.py:529
  417.0 92.4 %collective-permute-start.41 = (bf16[512,1024]{1,0:T(8,128)(2,1)}, bf16[512,1024]{1,0:T(8,128)(2,1)}, u32[]{:S(2)}, u32[]{:S(2)}) collective-permute-start(bf16[512,1024]{1,0:T(8,128)(2,1)} %get-tuple-element.103), channel_id=1, source_target_pairs={{0,4},{4,0},{8,12},{12,8},{16,20},{20,16},{24,28},{28,24},{1,5},{5... | collective-permute-start | bytes 3145736 | tf_op jit(solution)/shard_map/ppermute | solution.py:487
  470.6 35.3 %collective-permute-start.96 = (bf16[2,128,512]{1,2,0:T(8,128)(2,1)S(1)}, bf16[2,128,512]{1,2,0:T(8,128)(2,1)S(1)}, u32[]{:S(2)}, u32[]{:S(2)}) collective-permute-start(bf16[2,128,512]{1,2,0:T(8,128)(2,1)S(1)} %get-tuple-element.145), channel_id=1, source_target_pairs={{0,2},{1,3},{2,0},{3,1},{4,6},{5,7},{6,4},{7,5},{8,10},{9,11},{10,... | collective-permute-start | bytes 786440 | tf_op jit(solution)/shard_map/ppermute | solution.py:491
  577.2 43.9 %collective-permute-start.42 = (bf16[512,1024]{1,0:T(8,128)(2,1)}, bf16[512,1024]{1,0:T(8,128)(2,1)}, u32[]{:S(2)}, u32[]{:S(2)}) collective-permute-start(bf16[512,1024]{1,0:T(8,128)(2,1)} %select_convert_fusion), channel_id=1, source_target_pairs={{0,4},{4,0},{8,12},{12,8},{16,20},{20,16},{24,28},{28,24},{1,5},{5... | collective-permute-start | bytes 3145736 | tf_op jit(solution)/shard_map/ppermute | solution.py:487
  580.0 39.5 %collective-permute-start.52 = (bf16[2,128,1536]{1,2,0:T(8,128)(2,1)}, bf16[2,128,1536]{1,2,0:T(8,128)(2,1)}, u32[]{:S(2)}, u32[]{:S(2)}) collective-permute-start(bf16[2,128,1536]{1,2,0:T(8,128)(2,1)} %select_bitcast_fusion.12), channel_id=1, source_target_pairs={{0,8},{4,12},{8,0},{12,4},{16,24},{20,28},{24,16},{28,20},{1,9},{5... | collective-permute-start | bytes 2359304 | tf_op jit(solution)/shard_map/ppermute | solution.py:487
  (161 other events, 2192.3 us)
